TPU v7x, 512 devices: a whole 4x4x16 slice. The times are simulated.
512 devices in a mesh: flux: 16 (over z), obs: 32 (over y, x, core).
Axes of the slice: x: 4, y: 4, z: 16, core: 2. Of those that a mesh axis runs over, the one named last changes fastest.
Arguments:
- footprint: bfloat16 [4096, 4, 4, 2, 4096], P(('flux', 'obs')), may hold values from 0.00049972534 to 0.049804688
- obs_hour: int32 [4096, 4], P(('flux', 'obs')), may hold values from 0 to 3
- tile_list: int32 [4096, 4], P(('flux', 'obs')), may hold values from 0 to 511, as said below
- tile_row: int32 [512], replicated, may hold values from 0 to 511, as said below
- flux: bfloat16 [512, 5, 4096], P('flux'), may hold values from -6 to 6
- observed: float32 [4096, 4], P(('flux', 'obs')), may hold values from -18 to 18
- obs_var: float32 [4096, 4], P(('flux', 'obs')), may hold values from 0.5 to 4
Outputs:
- modeled: float32 [4096, 4], P(('flux', 'obs'))
- gradient: float32 [512, 5, 4096], P('flux', None, 'obs')
Inputs may be any that keep to these rules, and one draw needn't show every extreme that they name: `tile_row`: A permutation: every tile has its own storage row, and the row r lies on index r // 32 of flux. `tile_list`: among the 32 listed tiles of one device's 8 blocks, at most 4 have storage rows on one index of flux; on every device some index of flux gets exactly 4.
All inputs are finite; a program needn't handle non-finite values.
Results may differ from a plain program's by a relative error of at most 0.0019.
Values may be sent and summed in bfloat16 or wider, within the bound.
A program may use at most 64 MiB of HBM per device.

v0:
```python
import jax
import jax.numpy as jnp
from jax import lax
from jax.sharding import PartitionSpec as P


def hour_select(hour_rows, lag_count, hour_count):
    target = hour_rows[:, :, None] + jnp.arange(lag_count, dtype=jnp.int32)[None, None, :]
    return (target[..., None] == jnp.arange(hour_count, dtype=jnp.int32)).astype(jnp.float32)


def forward_terms(footprints, windows, select):
    products = jnp.einsum("nolc,nhc->nolh", footprints, windows, preferred_element_type=jnp.float32)
    return jnp.sum(products * select, axis=(2, 3))


def adjoint_terms(select, scaled, footprints):
    coefficient = (select * scaled.astype(jnp.float32)[:, :, None, None]).astype(jnp.bfloat16)
    return jnp.einsum("nolh,nolc->nhc", coefficient, footprints, preferred_element_type=jnp.float32)


def fetch_windows(flux, wanted):
    present = (wanted >= 0).astype(flux.dtype)
    rows_taken = jnp.take(flux, jnp.maximum(wanted, 0), axis=0)
    return rows_taken * present[:, None, None]


def accumulate(wanted, gradients, tile_count):
    onehot = (wanted[None, :] == jnp.arange(tile_count, dtype=jnp.int32)[:, None]).astype(
        jnp.float32
    )
    flattened = gradients.reshape(gradients.shape[0], gradients.shape[1] * gradients.shape[2])
    summed = jnp.dot(
        onehot, flattened, precision=lax.Precision.HIGHEST, preferred_element_type=jnp.float32
    )
    return summed.reshape(tile_count, gradients.shape[1], gradients.shape[2])


def shards(footprint, obs_hour, tile_list, tile_row, flux, observed, obs_var):
    owners = lax.axis_size("flux")
    block_count, slot_width, sounding_count, lag_count, cell_count = footprint.shape
    tile_count = flux.shape[0]
    hour_count = flux.shape[1]
    slot_count = block_count * slot_width
    capacity = 2 * slot_count // owners
    buffer_size = owners * capacity
    listed = tile_list.reshape(slot_count)
    table_hits = listed[:, None] == jnp.arange(tile_row.shape[0], dtype=jnp.int32)[None, :]
    storage = jnp.sum(jnp.where(table_hits, tile_row[None, :], 0), axis=1)
    owner_index = storage // tile_count
    local_index = storage % tile_count
    slot_iota = jnp.arange(slot_count, dtype=jnp.int32)
    earlier = (owner_index[:, None] == owner_index[None, :]) & (
        slot_iota[None, :] < slot_iota[:, None]
    )
    position = owner_index * capacity + jnp.sum(earlier.astype(jnp.int32), axis=1)
    matches = position[None, :] == jnp.arange(buffer_size, dtype=jnp.int32)[:, None]
    filled = jnp.any(matches, axis=1)
    source = jnp.sum(jnp.where(matches, slot_iota[None, :], 0), axis=1)
    requests = jnp.where(filled, local_index[source], -1).reshape(owners, capacity)
    select = hour_select(obs_hour, lag_count, hour_count)
    slot_select = jnp.broadcast_to(
        select[:, None], (block_count, slot_width, sounding_count, lag_count, hour_count)
    ).reshape(slot_count, sounding_count, lag_count, hour_count)
    slot_feet = footprint.reshape(slot_count, sounding_count, lag_count, cell_count)
    incoming = lax.all_to_all(requests, "flux", split_axis=0, concat_axis=0, tiled=True)
    served = fetch_windows(flux, incoming.reshape(buffer_size)).reshape(
        owners, capacity, hour_count, cell_count
    )
    arrived = lax.all_to_all(served, "flux", split_axis=0, concat_axis=0, tiled=True).reshape(
        buffer_size, hour_count, cell_count
    )
    slot_tiles = jnp.take(arrived, position, axis=0)
    partial_value = forward_terms(slot_feet, slot_tiles, slot_select).reshape(
        block_count, slot_width, sounding_count
    )
    modeled = jnp.sum(partial_value, axis=1)
    scaled = ((modeled - observed) / obs_var).astype(jnp.bfloat16)
    slot_scaled = jnp.broadcast_to(
        scaled[:, None], (block_count, slot_width, sounding_count)
    ).reshape(slot_count, sounding_count)
    gradients = adjoint_terms(slot_select, slot_scaled, slot_feet)
    outgoing = jnp.take(gradients, source, axis=0) * filled.astype(jnp.float32)[:, None, None]
    returned = lax.all_to_all(
        outgoing.reshape(owners, capacity, hour_count, cell_count),
        "flux",
        split_axis=0,
        concat_axis=0,
        tiled=True,
    )
    local_sum = accumulate(
        incoming.reshape(buffer_size),
        returned.reshape(buffer_size, hour_count, cell_count),
        tile_count,
    )
    gradient = lax.psum_scatter(local_sum, "obs", scatter_dimension=2, tiled=True)
    return (modeled, gradient)


def solution(mesh):
    placed = (
        P(("flux", "obs"), None, None, None, None),
        P(("flux", "obs"), None),
        P(("flux", "obs"), None),
        P(),
        P("flux", None, None),
        P(("flux", "obs"), None),
        P(("flux", "obs"), None),
    )
    return jax.shard_map(
        shards,
        mesh=mesh,
        in_specs=placed,
        out_specs=(P(("flux", "obs"), None), P("flux", None, "obs")),
        check_vma=False,
    )
```

profile of v0, /device:TPU:1, one launch (start us, length us, event | category | flops | bytes accessed | tf_op | source)
XLA Modules:
  0.0 571.0 jit_solution(4085145144219668630)
XLA Ops:
  7.2 0.0 copy-start
  7.2 0.9 copy.61
  8.1 0.1 eq.73
  8.2 0.9 select_reduce_fusion
  9.1 0.2 convert_reduce_fusion
  9.2 0.1 fusion.29
  9.3 0.1 select_reduce_fusion.1
  9.5 0.8 gather_fusion
  10.2 0.1 select_n.112
  10.3 26.8 %all_to_all.16 = s32[16,1,4]{2,1,0:T(1,128)S(1)} all-to-all(s32[16,1,4]{2,1,0:T(1,128)S(1)} %bitcast.78), channel_id=1, replica_groups=mesh['flux'=16,'obs'=32] {'flux'}, dimensions={0} | all-to-all | bytes 512 | tf_op jit(solution)/shard_map/all_to_all | solution.py:66
  37.2 0.1 copy.63
  37.3 0.1 copy.64
  37.4 0.1 copy.68
  37.5 0.1 copy.65
  37.5 0.1 reshape.252
  37.6 11.4 %gather_fusion.1 = bf16[64,5,4096]{2,0,1:T(8,128)(2,1)} fusion(bf16[32,5,4096]{2,0,1:T(8,128)(2,1)} %param.11, s32[1024]{0:T(1024)S(1)} %pad_clamp_fusion.1), kind=kCustom, calls=%fused_computation.1 | custom fusion | bytes 5243136 | tf_op jit(solution)/shard_map/jit(_take)/gather | solution.py:24
  49.1 5.1 gather.21
  54.2 4.6 fusion.4
  58.8 0.0 copy-start.2
  58.8 4.8 all-to-all-start.1
  63.6 0.1 reduce_sum.61
  63.6 0.0 copy-done.2
  63.6 0.1 copy.71
  63.7 0.1 reshape.241
  63.9 0.1 fusion.28
  64.0 113.6 %all-to-all-done.1 = bf16[16,4,5,4096]{3,1,2,0:T(4,128)(2,1)} async-done(((bf16[16,4,5,4096]{3,1,2,0:T(4,128)(2,1)}), bf16[16,4,5,4096]{3,1,2,0:T(4,128)(2,1)}, u32[]{:S(2)}, u32[]{:S(2)}) %all-to-all-start.1) | async-done | bytes 2621472 | tf_op jit(solution)/shard_map/all_to_all | solution.py:70
  177.6 5.5 copy.69
  183.1 4.2 gather_fusion.2
  187.3 0.0 copy-done
  187.3 0.0 copy-start.3
  187.4 0.0 copy-start.4
  187.4 3.7 fusion.21
  191.1 0.1 copy.82
  191.2 0.0 copy-done.3
  191.2 0.0 copy-done.4
  191.2 0.0 copy-start.1
  191.2 0.1 copy.83
  191.3 3.6 convolution_bitcast_fusion
  194.9 0.0 copy-done.1
  194.9 6.5 %gather_fusion.3 = f32[64,5,4096]{2,1,0:T(8,128)} fusion(f32[32,5,4096]{2,1,0:T(8,128)} %convolution_bitcast_fusion, s32[1024]{0:T(1024)S(1)} %pad_clamp_fusion.2), kind=kCustom, calls=%fused_computation.3 | custom fusion | bytes 10486016 | tf_op jit(solution)/shard_map/jit(_take)/gather | solution.py:83
  201.4 10.5 %fusion.3 = f32[16,4,5,4096]{3,1,2,0:T(4,128)} fusion(f32[16,4,5,4096]{3,2,1,0:T(8,128)} %bitcast.72, f32[16,4]{1,0:T(8,128)S(1)} %reshape.241, pred[16,4]{1,0:T(8,128)(4,1)S(1)} %compare_and_fusion), kind=kLoop, calls=%fused_computation.9 | loop fusion | flops 2621440 | bytes 10486080 | tf_op jit(solution)/shard_map/mul | solution.py:83
  211.9 11.2 %all-to-all-start.2 = ((f32[16,4,5,4096]{3,1,2,0:T(4,128)}), f32[16,4,5,4096]{3,1,2,0:T(4,128)}, u32[]{:S(2)}, u32[]{:S(2)}) async-start(f32[16,4,5,4096]{3,1,2,0:T(4,128)} %fusion.3), calls=%async_computation.2 | async-start | bytes 10485760 | tf_op jit(solution)/shard_map/all_to_all | solution.py:84
  223.1 0.3 reduce-scatter.2.cloned.1.call-start
  223.4 0.5 broadcast.307
  223.9 0.7 reduce.3
  224.6 0.1 reshape.239
  224.7 225.2 %all-to-all-done.2 = f32[16,4,5,4096]{3,1,2,0:T(4,128)} async-done(((f32[16,4,5,4096]{3,1,2,0:T(4,128)}), f32[16,4,5,4096]{3,1,2,0:T(4,128)}, u32[]{:S(2)}, u32[]{:S(2)}) %all-to-all-start.2) | async-done | bytes 5242912 | tf_op jit(solution)/shard_map/all_to_all | solution.py:84
  449.9 6.0 %copy.76 = f32[16,4,5,4096]{3,2,1,0:T(8,128)S(1)} copy(f32[16,4,5,4096]{3,1,2,0:T(4,128)} %all-to-all-done.2) | data formatting | bytes 10485760 | tf_op jit(solution)/shard_map/all_to_all | solution.py:84
  455.9 6.5 %fusion = f32[32,5,4096]{2,0,1:T(8,128)} fusion(s32[64]{0:T(128)S(1)} %reshape.239, f32[8,8,5,4096]{3,2,1,0:T(8,128)S(1)} %bitcast.73), kind=kOutput, calls=%fused_computation.5 | convolution fusion | flops 503318528 | bytes 7864576 | tf_op jit(solution)/shard_map/dot_general | solution.py:33
  462.5 0.0 reduce-scatter.2.cloned.1.call-update
  462.5 101.7 %reduce-scatter.2.cloned.1.call-done = f32[32,5,128]{2,0,1:T(8,128)} async-done(((f32[32,5,4096]{2,0,1:T(8,128)}), f32[32,5,128]{2,0,1:T(8,128)}) %reduce-scatter.2.cloned.1.call-update) | async-done | bytes 81936 | tf_op jit(solution)/shard_map/reduce_scatter | solution.py:96
  (17 shorter events, 0.2 us)
Async XLA Ops:
  7.2 180.2 %copy-start = (bf16[8,4,4,2,4096]{4,3,2,1,0:T(2,128)(2,1)S(1)}, bf16[8,4,4,2,4096]{4,3,2,1,0:T(2,128)(2,1)}, u32[]{:S(2)}) copy-start(bf16[8,4,4,2,4096]{4,3,2,1,0:T(2,128)(2,1)} %param.7) | copy-start | bytes 6291460
  58.8 4.9 copy-start.2
  58.8 118.8 %all-to-all-start.1 = ((bf16[16,4,5,4096]{3,1,2,0:T(4,128)(2,1)}), bf16[16,4,5,4096]{3,1,2,0:T(4,128)(2,1)}, u32[]{:S(2)}, u32[]{:S(2)}) async-start(bf16[16,4,5,4096]{3,1,2,0:T(4,128)(2,1)} %fusion.4), calls=%async_computation.1 | async-start | bytes 5242880 | tf_op jit(solution)/shard_map/all_to_all | solution.py:70
  187.3 3.9 copy-start.3
  187.4 3.9 copy-start.4
  191.2 3.7 copy-start.1
  211.9 238.0 %all-to-all-start.2 = ((f32[16,4,5,4096]{3,1,2,0:T(4,128)}), f32[16,4,5,4096]{3,1,2,0:T(4,128)}, u32[]{:S(2)}, u32[]{:S(2)}) async-start(f32[16,4,5,4096]{3,1,2,0:T(4,128)} %fusion.3), calls=%async_computation.2 | async-start | bytes 10485760 | tf_op jit(solution)/shard_map/all_to_all | solution.py:84
  223.1 341.0 %reduce-scatter.2.cloned.1.call-start = ((), (), s32[]{:S(2)}) async-start(), calls=%async_computation.4 | async-start | bytes 2703360 | tf_op jit(solution)/shard_map/reduce_scatter | solution.py:96
Sparse Core Ops, SparseCore 0:
  462.6 101.5 reduce-scatter.1
where the time goes:
time: 572 us; the launch traced here: 571 us
  waiting for transfers between devices  441 us (77%)
  local copies, waits for them, and re-layouts  42.1 us (7%)
  blocking collectives  26.8 us (5%)
  other arithmetic  17.2 us (3%)
  starting transfers between devices  16.2 us (3%)
  between operations  14.2 us (2%)
  matrix products  13.8 us (2%)
    all_to_all x1, waiting for transfers between devices, shards(): lax.all_to_all(outgoing.reshape(owners, capacity, hour_count, cell_count)...  225 us
    all_to_all x1, waiting for transfers between devices, shards(): lax.all_to_all(served, 'flux', split_axis=0, concat_axis=0, tiled=True)  114 us
    reduce_scatter x1, waiting for transfers between devices, shards(): lax.psum_scatter(local_sum, 'obs', scatter_dimension=2, tiled=True)  102 us
    all_to_all x1, blocking collectives, shards(): lax.all_to_all(requests, 'flux', split_axis=0, concat_axis=0, tiled=True)  26.8 us
    gather x2, local copies, waits for them, and re-layouts, fetch_windows(): rows_taken = jnp.take(flux, jnp.maximum(wanted, 0), axis=0)  16.5 us
  transfers between devices with their start and end apart: 3, of which 3 were waited for; matrix products, arithmetic and copies ran while one was open for 0% of the time, Pallas kernels for 0%

commit v1 on v0

v1 whole, which is shorter than its diff:
```python
import jax
import jax.numpy as jnp
from jax import lax
from jax.sharding import PartitionSpec as P


def shards(footprint, obs_hour, tile_list, tile_row, flux, observed, obs_var):
    columns = lax.axis_size("obs")
    block_count, slot_width, sounding_count, lag_count, cell_count = footprint.shape
    tile_count, hour_count, _ = flux.shape
    chunk = cell_count // columns
    me = lax.axis_index("obs")
    table_hits = tile_list[..., None] == jnp.arange(tile_row.shape[0], dtype=jnp.int32)
    storage = jnp.sum(jnp.where(table_hits, tile_row, 0), axis=-1)
    numbers = jnp.concatenate(
        [storage.astype(jnp.float32), obs_hour.astype(jnp.float32), observed, obs_var], axis=1
    )
    numbers = lax.all_gather(numbers, "obs", axis=0, tiled=True)
    rows = numbers[:, 0:4].astype(jnp.int32)
    hours = numbers[:, 4:8].astype(jnp.int32)
    own_flux = lax.dynamic_slice_in_dim(flux, me * chunk, chunk, axis=2)
    all_flux = lax.all_gather(own_flux, "flux", axis=0, tiled=True)
    total = all_flux.shape[0]
    feet = footprint.reshape(-1, columns, chunk).transpose(1, 0, 2)
    feet = lax.all_to_all(feet, "obs", split_axis=0, concat_axis=0, tiled=True)
    blocks = block_count * columns
    feet = feet.reshape(blocks, slot_width, sounding_count, lag_count, chunk)
    onehot = rows.reshape(-1)[:, None] == jnp.arange(total, dtype=jnp.int32)[None, :]
    windows = jnp.dot(
        onehot.astype(jnp.bfloat16),
        all_flux.reshape(total, hour_count * chunk),
        preferred_element_type=jnp.float32,
    ).reshape(blocks, slot_width, hour_count, chunk)
    hour_at = hours[:, :, None] + jnp.arange(lag_count, dtype=jnp.int32)
    select = hour_at[..., None] == jnp.arange(hour_count, dtype=jnp.int32)
    picked = 0.0
    for h in range(hour_count):
        picked = picked + jnp.where(
            select[:, None, :, :, h, None], windows[:, :, None, None, h, :], 0.0
        )
    partial_value = jnp.sum(feet.astype(jnp.float32) * picked, axis=(1, 3, 4))
    modeled_all = lax.psum(partial_value, "obs")
    scaled = ((modeled_all - numbers[:, 8:12]) / numbers[:, 12:16]).astype(jnp.bfloat16)
    modeled = lax.dynamic_slice_in_dim(modeled_all, me * block_count, block_count, axis=0)
    coefficient = jnp.where(select, scaled.astype(jnp.float32)[:, :, None, None], 0.0)
    terms = []
    for h in range(hour_count):
        terms.append(
            jnp.sum(feet.astype(jnp.float32) * coefficient[:, None, :, :, h, None], axis=(2, 3))
        )
    terms = jnp.stack(terms, axis=2).reshape(blocks * slot_width, hour_count * chunk)
    high = terms.astype(jnp.bfloat16)
    low = (terms - high.astype(jnp.float32)).astype(jnp.bfloat16)
    spread = onehot.astype(jnp.bfloat16)
    summed = lax.dot_general(
        spread, high, (((0,), (0,)), ((), ())), preferred_element_type=jnp.float32
    ) + lax.dot_general(spread, low, (((0,), (0,)), ((), ())), preferred_element_type=jnp.float32)
    gradient = lax.psum_scatter(
        summed.reshape(total, hour_count, chunk), "flux", scatter_dimension=0, tiled=True
    )
    return modeled, gradient


def solution(mesh):
    placed = (
        P(("flux", "obs"), None, None, None, None),
        P(("flux", "obs"), None),
        P(("flux", "obs"), None),
        P(),
        P("flux", None, None),
        P(("flux", "obs"), None),
        P(("flux", "obs"), None),
    )
    return jax.shard_map(
        shards,
        mesh=mesh,
        in_specs=placed,
        out_specs=(P(("flux", "obs"), None), P("flux", None, "obs")),
        check_vma=False,
    )
```

time: 572 us -> 358 us (0.63)
  the two profiles are of different devices: /device:TPU:1 before, /device:TPU:8 now
where the time goes in v1:
time: 358 us; the launch traced here: 356 us
  blocking collectives  135 us (38%)
  local copies, waits for them, and re-layouts  82.3 us (23%)
  waiting for transfers between devices  72.9 us (20%)
  other arithmetic  31.1 us (9%)
  between operations  14.4 us (4%)
  matrix products  10.1 us (3%)
  starting transfers between devices  9.58 us (3%)
    reduce_scatter x1, waiting for transfers between devices, shards(): lax.psum_scatter(summed.reshape(total, hour_count, chunk), 'flux', scatte...  72.9 us
    psum x1, blocking collectives, shards(): modeled_all = lax.psum(partial_value, 'obs')  53.2 us
    broadcast_in_dim x27, local copies, waits for them, and re-layouts, shards(): jnp.where(select[:, None, :, :, h, None], windows[:, :, None, None, h, :]...  43.3 us
    all_gather x1, blocking collectives, shards(): numbers = lax.all_gather(numbers, 'obs', axis=0, tiled=True)  42.4 us
    all_gather x1, blocking collectives, shards(): all_flux = lax.all_gather(own_flux, 'flux', axis=0, tiled=True)  39.7 us
    reduce_sum x1, other arithmetic, shards(): jnp.sum(feet.astype(jnp.float32) * coefficient[:, None, :, :, h, None], a...  18.6 us
    reduce_sum x2, other arithmetic, shards(): partial_value = jnp.sum(feet.astype(jnp.float32) * picked, axis=(1, 3, 4))  10.7 us
    another operation x1, local copies, waits for them, and re-layouts, shards(): jnp.stack(terms, axis=2).reshape(blocks * slot_width, hour_count * chunk)  10.5 us
  transfers between devices with their start and end apart: 2, of which 1 were waited for; matrix products, arithmetic and copies ran while one was open for 14% of the time, Pallas kernels for 0%

profile of v1, /device:TPU:8, one launch (start us, length us, event | category | flops | bytes accessed | tf_op | source)
XLA Modules:
  0.0 355.8 jit_solution(15153389452616925642)
XLA Ops:
  7.2 3.4 reshape.75
  10.7 2.2 copy.126
  12.8 9.5 %all-to-all-start = ((bf16[32,256,128]{2,1,0:T(8,128)(2,1)}), bf16[32,256,128]{2,1,0:T(8,128)(2,1)S(1)}, u32[]{:S(2)}, u32[]{:S(2)}) async-start(bf16[32,256,128]{2,1,0:T(8,128)(2,1)} %copy.126), calls=%async_computation | async-start | bytes 4194304 | tf_op jit(solution)/shard_map/all_to_all | solution.py:25
  22.4 0.0 reduce-scatter.2.cloned.1.call-start
  22.5 0.2 select_reduce_fusion
  22.7 0.1 copy.127
  22.8 42.4 %all_gather.6 = f32[256,16]{1,0:T(8,128)S(1)} all-gather(f32[8,16]{1,0:T(8,128)S(1)} %copy.127), channel_id=1, replica_groups=mesh['flux'=16,'obs'=32] {'obs'}, dimensions={0}, use_global_device_ids=true | all-gather | bytes 16896 | tf_op jit(solution)/shard_map/all_gather | solution.py:18
  65.2 0.9 fusion.14
  66.1 0.7 eq.73
  66.8 0.7 copy.130
  67.5 1.6 copy.157
  69.1 1.0 copy.156
  70.1 1.6 copy.158
  71.7 0.6 slice_bitcast_fusion.14
  72.3 1.0 copy.129
  73.2 1.6 copy.139
  74.8 1.6 copy.137
  76.4 0.9 copy.135
  77.3 0.9 copy.133
  78.3 2.0 broadcast_in_dim.153
  80.3 2.6 broadcast_in_dim.154
  82.9 2.0 broadcast_in_dim.160
  85.0 3.2 broadcast_in_dim.161
  88.2 2.0 broadcast_in_dim.167
  90.2 3.2 broadcast_in_dim.168
  93.5 2.0 broadcast_in_dim.174
  95.5 3.2 broadcast_in_dim.175
  98.7 1.1 broadcast_in_dim.145
  99.9 2.6 broadcast_in_dim.146
  102.5 39.7 %all_gather.7 = bf16[512,5,128]{2,0,1:T(8,128)(2,1)} all-gather(bf16[32,5,128]{2,0,1:T(8,128)(2,1)S(1)} %constant_dynamic-slice_fusion), channel_id=1, replica_groups=mesh['flux'=16,'obs'=32] {'flux'}, dimensions={0}, use_global_device_ids=true | all-gather | bytes 696320 | tf_op jit(solution)/shard_map/all_gather | solution.py:22
  142.3 2.2 copy.131
  144.4 2.2 fusion.4
  146.6 0.2 slice_bitcast_fusion.4
  146.8 1.1 copy.132
  148.0 1.1 copy.140
  149.1 1.1 copy.138
  150.3 1.2 copy.136
  151.4 1.1 copy.134
  152.5 2.2 broadcast_in_dim.157
  154.8 1.1 broadcast_in_dim.164
  155.9 1.1 broadcast_in_dim.171
  157.0 1.1 broadcast_in_dim.178
  158.1 1.1 broadcast_in_dim.149
  159.2 8.6 %multiply_reduce_fusion.5 = f32[32,256]{1,0:T(8,128)S(1)} fusion(f32[32,256,128]{2,1,0:T(8,128)S(1)} %bitcast.76, f32[32,256,128]{2,1,0:T(8,128)S(1)} %bitcast.75, f32[32,256,128]{2,1,0:T(8,128)S(1)} %bitcast.74, f32[32,256,128]{2,1,0:T(8,128)S(1)} %bitcast.73, f32[32,256,128]{2,1,0:T(8,128)S(1)} %bitcast.77, pred[32,256]{1,0:T(8,128)(4,1)S(1)} %copy-done.7, ...), kind=kLoop, calls=%fused_computation.5 | loop fusion | flops 12574720 | bytes 23142400 | tf_op jit(solution)/shard_map/reduce_sum | solution.py:41
  167.8 4.0 %reduce_sum.72 = f32[256,4,4,2]{3,2,1,0:T(4,128)} reshape(f32[32,256]{1,0:T(8,128)S(1)} %multiply_reduce_fusion.5) | data formatting | bytes 65536 | tf_op jit(solution)/shard_map/reduce_sum | solution.py:41
  171.9 2.1 reduce_sum.73
  174.0 0.1 copy.143
  174.0 53.2 %psum.7 = f32[256,4]{0,1:T(4,128)S(1)} all-reduce(f32[256,4]{0,1:T(4,128)S(1)} %copy.143), channel_id=1, replica_groups=mesh['flux'=16,'obs'=32] {'obs'}, use_global_device_ids=true, to_apply=%region_3.4 | all-reduce | flops 1024 | bytes 8192 | tf_op jit(solution)/shard_map/psum | solution.py:42
  227.3 0.7 fusion.13
  228.0 1.0 copy.146
  229.0 1.0 copy.150
  230.0 1.0 copy.149
  231.1 1.0 copy.148
  232.1 1.0 copy.147
  233.2 18.6 %multiply_reduce_fusion = (f32[256,4,128]{2,1,0:T(4,128)}, f32[256,4,128]{2,1,0:T(4,128)}, f32[256,4,128]{2,1,0:T(4,128)}, f32[256,4,128]{2,1,0:T(4,128)}, f32[256,4,128]{2,1,0:T(4,128)}) fusion(f32[256,4,2]{2,1,0:T(4,128)} %copy.150, f32[256,4,2]{2,1,0:T(4,128)} %copy.149, f32[256,4,2]{2,1,0:T(4,128)} %copy.148, f32[256,4,2]{2,1,0:T(4,128)} %copy.147, ...), kind=kLoop, calls=%fused_computation | loop fusion | flops 10878976 | bytes 4759552 | tf_op jit(solution)/shard_map/reduce_sum | solution.py:49
  251.8 10.5 %stack.23 = f32[256,4,5,128]{3,2,1,0:T(8,128)} concatenate(f32[256,4,1,128]{3,2,1,0:T(1,128)} %bitcast.86, f32[256,4,1,128]{3,2,1,0:T(1,128)} %bitcast.85, f32[256,4,1,128]{3,2,1,0:T(1,128)} %bitcast.84, f32[256,4,1,128]{3,2,1,0:T(1,128)} %bitcast.83, f32[256,4,1,128]{3,2,1,0:T(1,128)} %bitcast.82), dimensions={2} | concatenate | bytes 5242880 | tf_op jit(solution)/shard_map/stack | solution.py:51
  262.3 3.5 fusion.1
  265.8 4.4 %fusion.6 = f32[512,640]{1,0:T(8,128)} fusion(f32[512,640]{1,0:T(8,128)S(1)} %fusion.1, f32[128,8,5,128]{3,2,1,0:T(8,128)} %bitcast.81, s32[1024]{0:T(1024)S(1)} %copy-done.9), kind=kOutput, calls=%fused_computation.15 | convolution fusion | flops 671940608 | bytes 5246976 | tf_op jit(solution)/shard_map/dot_general | solution.py:55
  270.2 1.7 copy.151
  271.9 1.8 copy.152
  273.8 0.0 reduce-scatter.2.cloned.1.call-update
  273.8 0.7 constant_dynamic-slice_fusion.1
  274.4 72.9 %reduce-scatter.2.cloned.1.call-done = f32[32,5,128]{2,1,0:T(8,128)} async-done(((f32[512,5,128]{2,1,0:T(8,128)}), f32[32,5,128]{2,1,0:T(8,128)}) %reduce-scatter.2.cloned.1.call-update) | async-done | bytes 81936 | tf_op jit(solution)/shard_map/reduce_scatter | solution.py:58
  347.4 1.6 copy.153
  (40 shorter events, 0.2 us)
Async XLA Ops:
  7.2 95.3 %copy-start = (bf16[32,5,4096]{2,0,1:T(8,128)(2,1)S(1)}, bf16[32,5,4096]{2,0,1:T(8,128)(2,1)}, u32[]{:S(2)}) copy-start(bf16[32,5,4096]{2,0,1:T(8,128)(2,1)} %param.11) | copy-start | bytes 3932164
  10.6 11.8 %copy-start.12 = (s32[8,4]{0,1:T(4,128)S(1)}, s32[8,4]{0,1:T(4,128)}, u32[]{:S(2)}) copy-start(s32[8,4]{0,1:T(4,128)} %param.8) | copy-start | bytes 388
  10.6 11.8 %copy-start.10 = (s32[512]{0:T(512)S(1)}, s32[512]{0:T(512)}, u32[]{:S(2)}) copy-start(s32[512]{0:T(512)} %param.10) | copy-start | bytes 6148
  10.6 11.8 %copy-start.11 = (s32[8,4]{0,1:T(4,128)S(1)}, s32[8,4]{0,1:T(4,128)}, u32[]{:S(2)}) copy-start(s32[8,4]{0,1:T(4,128)} %param.9) | copy-start | bytes 388
  10.7 12.1 %copy-start.13 = (f32[8,4]{0,1:T(4,128)S(1)}, f32[8,4]{0,1:T(4,128)}, u32[]{:S(2)}) copy-start(f32[8,4]{0,1:T(4,128)} %param.13) | copy-start | bytes 388
  10.7 12.1 %copy-start.14 = (f32[8,4]{0,1:T(4,128)S(1)}, f32[8,4]{0,1:T(4,128)}, u32[]{:S(2)}) copy-start(f32[8,4]{0,1:T(4,128)} %param.12) | copy-start | bytes 388
  12.8 139.7 %all-to-all-start = ((bf16[32,256,128]{2,1,0:T(8,128)(2,1)}), bf16[32,256,128]{2,1,0:T(8,128)(2,1)S(1)}, u32[]{:S(2)}, u32[]{:S(2)}) async-start(bf16[32,256,128]{2,1,0:T(8,128)(2,1)} %copy.126), calls=%async_computation | async-start | bytes 4194304 | tf_op jit(solution)/shard_map/all_to_all | solution.py:25
  22.4 325.0 %reduce-scatter.2.cloned.1.call-start = ((), (), s32[]{:S(2)}) async-start(), calls=%async_computation.2 | async-start | bytes 2228224 | tf_op jit(solution)/shard_map/reduce_scatter | solution.py:58
  152.5 2.2 copy-start.4
  152.5 3.3 copy-start.3
  154.8 2.2 copy-start.2
  155.9 2.2 copy-start.1
  157.0 2.2 copy-start.5
  157.0 2.2 copy-start.6
  157.0 2.2 copy-start.7
  167.8 59.4 %copy-start.8 = (f32[256,4]{0,1:T(4,128)S(1)}, f32[256,4]{0,1:T(4,128)}, u32[]{:S(2)}) copy-start(f32[256,4]{0,1:T(4,128)} %copy.157) | copy-start | bytes 12292
  251.8 10.5 %copy-start.9 = (s32[1024]{0:T(1024)S(1)}, s32[1024]{0:T(1024)}, u32[]{:S(2)}) copy-start(s32[1024]{0:T(1024)} %eq.73) | copy-start | bytes 12292
Sparse Core Ops, SparseCore 0:
  273.9 73.4 reduce-scatter.1

commit v2 on v1

v2 whole, which is shorter than its diff:
```python
import functools

import jax
import jax.numpy as jnp
from jax import lax
from jax.experimental import pallas as pl
from jax.experimental.pallas import tpu as pltpu
from jax.sharding import PartitionSpec as P

MESH = pl.DeviceIdType.MESH
LANES = 128
ROW = 4


def kernel(
    nz, nobs, hours, feet, flux, meta, mod, grad,
    held, window, metas, pairs, onehot, spread, near, parts, total, high, low, mine, down, up,
    local_sem, ring_send, ring_recv, meta_send, meta_recv, feet_send, feet_recv,
    part_send, part_recv, down_send, down_recv, up_send, up_recv,
):
    f32, bf16 = jnp.float32, jnp.bfloat16
    chips = nobs // 2
    tiles = flux.shape[1]
    blocks = 8
    width = 2 * blocks
    slots = chips * width
    z = lax.axis_index("flux")
    me = lax.axis_index("obs")
    chip, core = me // 2, lax.rem(me, 2)
    y, x = chip // ROW, lax.rem(chip, ROW)
    above, below = lax.rem(z + 1, nz), lax.rem(z + nz - 1, nz)
    plus = nz // 2
    minus = nz - 1 - plus

    def target(t):
        c = t // 2
        there = lax.rem(y + c // ROW, chips // ROW) * ROW + lax.rem(x + lax.rem(c, ROW), ROW)
        return there * 2 + lax.rem(core + t, 2)

    def source_chip(c):
        return lax.rem(y + chips // ROW - c // ROW, chips // ROW) * ROW + lax.rem(
            x + ROW - lax.rem(c, ROW), ROW
        )

    def source(t):
        return source_chip(t // 2) * 2 + lax.rem(core + t, 2)

    def place(i):
        return held.at[i // 2, :, pl.ds(lax.rem(i, 2) * 64, 64), :]

    def remote(src, dst, send, recv, to):
        return pltpu.make_async_remote_copy(
            src_ref=src, dst_ref=dst, send_sem=send, recv_sem=recv,
            device_id=to, device_id_type=MESH,
        )

    def feet_copy(t):
        to = target(t)
        return remote(feet.at[to], place(me), feet_send.at[t], feet_recv.at[t], (z, to))

    def feet_arrival(t):
        return remote(feet.at[me], place(source(t)), feet_send.at[t], feet_recv.at[t], (z, target(t)))

    def meta_copy(t, i):
        return remote(meta, metas.at[i], meta_send.at[t], meta_recv.at[t], (z, target(t)))

    def part_copy(t, i):
        return remote(parts.at[me], parts.at[i], part_send.at[t], part_recv.at[t], (z, target(t)))

    def ring_copy(way, s, origin):
        at = window.at[:, pl.ds(lax.rem(origin + nz, nz) * tiles, tiles), :]
        return remote(at, at, ring_send.at[way, s], ring_recv.at[way, s], (above if way == 0 else below, me))

    own_feet = pltpu.make_async_copy(feet.at[me], place(me), local_sem.at[0])
    own_flux = pltpu.make_async_copy(
        flux.at[:, :, pl.ds(me * LANES, LANES)],
        window.at[:, pl.ds(z * tiles, tiles), :],
        local_sem.at[1],
    )
    own_feet.start()
    own_flux.start()
    metas[me] = meta[...]

    barrier = pltpu.get_barrier_semaphore()

    @pl.loop(1, nobs)
    def _(t):
        pl.semaphore_signal(barrier, inc=1, device_id=(z, target(t)), device_id_type=MESH)

    pl.semaphore_signal(barrier, inc=1, device_id=(above, me), device_id_type=MESH)
    pl.semaphore_signal(barrier, inc=1, device_id=(below, me), device_id_type=MESH)
    own_flux.wait()
    pl.semaphore_wait(barrier, nobs + 1)

    ring_copy(0, 0, z).start()
    if minus > 0:
        ring_copy(1, 0, z).start()

    @pl.loop(1, nobs)
    def _(t):
        meta_copy(t, me).start()
        feet_copy(t).start()

    for s in range(1, plus):
        ring_copy(0, s - 1, z - s).wait_recv()
        ring_copy(0, s, z - s).start()
        if s < minus:
            ring_copy(1, s - 1, z + s).wait_recv()
            ring_copy(1, s, z + s).start()
    ring_copy(0, plus - 1, z - plus).wait_recv()
    if minus > 0:
        ring_copy(1, minus - 1, z + minus).wait_recv()

    @pl.loop(1, nobs)
    def _(t):
        meta_copy(t, source(t)).wait_recv()

    lane = lax.broadcasted_iota(jnp.int32, (8, LANES), 1)
    per_half = nobs // 2
    halves = []
    for half in range(2):
        gathered = jnp.zeros((8, LANES), f32)
        for i in range(per_half):
            gathered = jnp.where(lane // blocks == i, metas[half * per_half + i], gathered)
        halves.append(gathered)

    @pl.loop(0, chips)
    def _(g):
        pairs[g] = jnp.where(lane < 64, metas[2 * g], metas[2 * g + 1])

    count = nz * tiles
    for half in range(2):
        upright = halves[half].T
        for k in range(4):
            at = k * slots + half * LANES
            across = halves[half][4 + k : 5 + k, :]
            tile_at = lax.broadcasted_iota(jnp.int32, (count, LANES), 0).astype(f32)
            spread[:, at : at + LANES] = jnp.where(tile_at == across, 1.0, 0.0).astype(bf16)
            along = upright[:, 4 + k : 5 + k]
            tile_on = lax.broadcasted_iota(jnp.int32, (LANES, count), 1).astype(f32)
            onehot[at : at + LANES, :] = jnp.where(tile_on == along, 1.0, 0.0).astype(bf16)

    @pl.loop(0, 4)
    def _(k):
        begin = pl.multiple_of(k * slots, LANES)
        pick = onehot[pl.ds(begin, slots), :]
        for h in range(hours):
            near[h, pl.ds(begin, slots), :] = jnp.dot(
                pick, window[h], preferred_element_type=f32
            ).astype(bf16)

    mask_row = lax.broadcasted_iota(jnp.int32, (hours * width, LANES), 0)
    mask_lane = lax.broadcasted_iota(jnp.int32, (hours * width, LANES), 1)
    same_block = lax.rem(mask_row, width) == mask_lane // 8
    hour_of = (mask_row // width).astype(f32)

    def mask(g):
        return same_block & (hour_of == pairs[g, 0:1, :])

    def group_feet(g):
        return jnp.concatenate([held[g, k] for k in range(4)], axis=1)

    own_feet.wait()

    @pl.loop(0, chips)
    def _(c):
        @pl.when(c > 0)
        def _():
            feet_arrival(2 * c).wait_recv()

        feet_arrival(2 * c + 1).wait_recv()
        g = source_chip(c)
        flux_rows = []
        for k in range(4):
            begin = pl.multiple_of(k * slots + g * width, width)
            flux_rows.append(
                jnp.concatenate([near[h, pl.ds(begin, width), :] for h in range(hours)], axis=0)
            )
        products = lax.dot_general(
            jnp.concatenate(flux_rows, axis=1), group_feet(g),
            (((1,), (1,)), ((), ())), preferred_element_type=f32,
        )
        parts[me, pl.ds(g, 1), :] = jnp.sum(
            jnp.where(mask(g), products, 0.0), axis=0, keepdims=True
        )

    @pl.loop(1, nobs)
    def _(t):
        part_copy(t, me).start()

    @pl.loop(1, nobs)
    def _(t):
        part_copy(t, source(t)).wait_recv()

    summed = parts[0]
    for i in range(1, nobs):
        summed = summed + parts[i]
    even = lax.rem(lax.broadcasted_iota(jnp.int32, (chips, LANES), 1), 2) == 0
    total[...] = summed + jnp.where(
        even, pltpu.roll(summed, LANES - 1, 1), pltpu.roll(summed, 1, 1)
    )
    mod[...] = jnp.broadcast_to(total[pl.ds(chip, 1), :], mod.shape)

    @pl.loop(0, chips)
    def _(g):
        misfit = (total[pl.ds(g, 1), :] - pairs[g, 1:2, :]) / pairs[g, 2:3, :]
        scaled = misfit.astype(bf16).astype(f32)
        coefficient = jnp.where(mask(g), scaled, 0.0).astype(bf16)
        terms = jnp.dot(coefficient, group_feet(g), preferred_element_type=f32)
        upper = terms.astype(bf16)
        lower = (terms - upper.astype(f32)).astype(bf16)
        for k in range(4):
            begin = pl.multiple_of(k * slots + g * width, width)
            for h in range(hours):
                cut = (slice(h * width, (h + 1) * width), slice(k * LANES, (k + 1) * LANES))
                high[pl.ds(begin, width), h * LANES : (h + 1) * LANES] = upper[cut]
                low[pl.ds(begin, width), h * LANES : (h + 1) * LANES] = lower[cut]

    @pl.loop(0, count // LANES)
    def _(q):
        pick = spread[pl.ds(pl.multiple_of(q * LANES, LANES), LANES), :]
        rows = jnp.dot(pick, high[...], preferred_element_type=f32) + jnp.dot(
            pick, low[...], preferred_element_type=f32
        )
        for i in range(LANES // tiles):
            for h in range(hours):
                mine[q * (LANES // tiles) + i, h] = rows[
                    i * tiles : (i + 1) * tiles, h * LANES : (h + 1) * LANES
                ]

    def down_copy(s, p):
        at = lax.rem(z + nz - plus + s, nz)
        if isinstance(s, int) and s == 0:
            src = mine.at[at, p]
        else:
            src = down.at[s - 1, p]
        return remote(src, down.at[s, p], down_send.at[s, p], down_recv.at[s, p], (below, me))

    def up_copy(s, p):
        at = lax.rem(z + minus - s + nz, nz)
        if isinstance(s, int) and s == 0:
            src = mine.at[at, p]
        else:
            src = up.at[s - 1, p]
        return remote(src, up.at[s, p], up_send.at[s, p], up_recv.at[s, p], (above, me))

    def down_step(s, p):
        down_copy(s - 1 if not isinstance(s, int) else max(s - 1, 0), p).wait_recv()
        down[s - 1, p] += mine[lax.rem(z + nz - plus + s, nz), p]
        down_copy(s, p).start()

    def up_step(s, p):
        up_copy(s - 1 if not isinstance(s, int) else max(s - 1, 0), p).wait_recv()
        up[s - 1, p] += mine[lax.rem(z + minus - s + nz, nz), p]
        up_copy(s, p).start()

    for p in range(hours):
        down_copy(0, p).start()
        if minus > 0:
            up_copy(0, p).start()
    for s in range(1, plus):
        for p in range(hours):
            down_step(s, p)
            if s < minus:
                up_step(s, p)
    for p in range(hours):
        down_copy(plus - 1, p).wait_recv()
        value = mine[z, p] + down[plus - 1, p]
        if minus > 0:
            up_copy(minus - 1, p).wait_recv()
            value = value + up[minus - 1, p]
        grad[p] = value

    for s in range(plus):
        ring_copy(0, s, z).wait_send()
        for p in range(hours):
            down_copy(s, p).wait_send()
    for s in range(minus):
        ring_copy(1, s, z).wait_send()
        for p in range(hours):
            up_copy(s, p).wait_send()

    @pl.loop(1, nobs)
    def _(t):
        meta_copy(t, me).wait_send()
        feet_copy(t).wait_send()
        part_copy(t, me).wait_send()


def shards(footprint, obs_hour, tile_list, tile_row, flux, observed, obs_var):
    nobs, nz = lax.axis_size("obs"), lax.axis_size("flux")
    block_count, slot_width, sounding_count, lag_count, cell_count = footprint.shape
    tile_count, hour_count, _ = flux.shape
    me = lax.axis_index("obs")
    f32, bf16 = jnp.float32, jnp.bfloat16
    table_hits = tile_list[..., None] == jnp.arange(tile_row.shape[0], dtype=jnp.int32)
    storage = jnp.sum(jnp.where(table_hits, tile_row, 0), axis=-1).astype(f32)

    def wide(values):
        return jnp.tile(jnp.repeat(values.reshape(1, -1), lag_count, axis=1), (1, 2))

    lags = (jnp.arange(LANES) % lag_count).astype(f32)[None]
    meta = jnp.concatenate(
        [
            wide(obs_hour.astype(f32)) + lags,
            wide(observed),
            wide(obs_var),
            jnp.zeros((1, LANES), f32),
            jnp.tile(storage.T, (1, LANES // block_count)),
        ],
        axis=0,
    )
    feet = footprint.reshape(
        block_count, slot_width, sounding_count * lag_count, nobs, LANES
    ).transpose(3, 1, 0, 2, 4).reshape(nobs, slot_width, 64, LANES)
    chips, count, slots = nobs // 2, nz * tile_count, nobs * block_count
    plus = nz // 2
    minus = max(nz - 1 - plus, 1)
    dma = pltpu.SemaphoreType.DMA
    mod, grad = pl.pallas_call(
        functools.partial(kernel, nz, nobs, hour_count),
        out_shape=(
            jax.ShapeDtypeStruct((8, LANES), f32),
            jax.ShapeDtypeStruct((hour_count, tile_count, LANES), f32),
        ),
        in_specs=[
            pl.BlockSpec(memory_space=pl.ANY),
            pl.BlockSpec(memory_space=pl.ANY),
            pl.BlockSpec(memory_space=pltpu.VMEM),
        ],
        out_specs=(pl.BlockSpec(memory_space=pltpu.VMEM),) * 2,
        scratch_shapes=[
            pltpu.VMEM((chips, slot_width, LANES, LANES), bf16),
            pltpu.VMEM((hour_count, count, LANES), bf16),
            pltpu.VMEM((nobs, 8, LANES), f32),
            pltpu.VMEM((chips, 8, LANES), f32),
            pltpu.VMEM((slots * slot_width, count), bf16),
            pltpu.VMEM((count, slots * slot_width), bf16),
            pltpu.VMEM((hour_count, slots * slot_width, LANES), bf16),
            pltpu.VMEM((nobs, chips, LANES), f32),
            pltpu.VMEM((chips, LANES), f32),
            pltpu.VMEM((slots * slot_width, hour_count * LANES), bf16),
            pltpu.VMEM((slots * slot_width, hour_count * LANES), bf16),
            pltpu.VMEM((nz, hour_count, tile_count, LANES), f32),
            pltpu.VMEM((plus, hour_count, tile_count, LANES), f32),
            pltpu.VMEM((minus, hour_count, tile_count, LANES), f32),
            dma((2,)),
            dma((2, plus)),
            dma((2, plus)),
            dma((nobs,)),
            dma((nobs,)),
            dma((nobs,)),
            dma((nobs,)),
            dma((nobs,)),
            dma((nobs,)),
            dma((plus, hour_count)),
            dma((plus, hour_count)),
            dma((minus, hour_count)),
            dma((minus, hour_count)),
        ],
        compiler_params=pltpu.CompilerParams(
            collective_id=0, has_side_effects=True, vmem_limit_bytes=40 << 20
        ),
        name="transport",
    )(feet, flux.transpose(1, 0, 2), meta)
    own = lax.dynamic_slice_in_dim(mod[0], lax.rem(me, 2) * 64, 64)
    modeled = own.reshape(block_count, sounding_count, lag_count)[:, :, 0]
    return modeled, grad.transpose(1, 0, 2)


def solution(mesh):
    placed = (
        P(("flux", "obs"), None, None, None, None),
        P(("flux", "obs"), None),
        P(("flux", "obs"), None),
        P(),
        P("flux", None, None),
        P(("flux", "obs"), None),
        P(("flux", "obs"), None),
    )
    return jax.shard_map(
        shards,
        mesh=mesh,
        in_specs=placed,
        out_specs=(P(("flux", "obs"), None), P("flux", None, "obs")),
        check_vma=False,
    )
```

time: 358 us -> 108 us (0.30)
  blocking collectives: 135 us -> 0 us
  Pallas kernels: 0 us -> 97.2 us
  waiting for transfers between devices: 72.9 us -> 0 us
  local copies, waits for them, and re-layouts: 82.3 us -> 9.97 us
  other arithmetic: 31.1 us -> 0.24 us
  between operations: 14.4 us -> 0.77 us
  matrix products: 10.1 us -> 0 us
  starting transfers between devices: 9.58 us -> 0 us
    pallas_call x0 -> x1, Pallas kernels: none -> 97.2 us  [shards(): pl.pallas_call(functools.partial(kernel, nz, nobs, hour_count), out_shape...]
    all_gather x2 -> x0, blocking collectives: 82.1 us -> none  [the longest x1 42.4 us: shards(): numbers = lax.all_gather(numbers, 'obs', axis=0, tiled=True)]
    reduce_scatter x1 -> x0, waiting for transfers between devices: 72.9 us -> none  [shards(): lax.psum_scatter(summed.reshape(total, hour_count, chunk), 'flux', scatte...]
    psum x1 -> x0, blocking collectives: 53.2 us -> none  [shards(): modeled_all = lax.psum(partial_value, 'obs')]
    broadcast_in_dim x27 -> x7, local copies, waits for them, and re-layouts: 43.3 us -> 0.55 us  [the longest x6 0.55 us: wide(): jnp.repeat(values.reshape(1, -1), lag_count, axis=1)]
    reduce_sum x4 -> x1, other arithmetic: 29.5 us -> 0.22 us  [shards(): storage = jnp.sum(jnp.where(table_hits, tile_row, 0), axis=-1).astype(f32)]
    another operation x1 -> x8, local copies, waits for them, and re-layouts: 10.5 us -> 0.35 us  [the longest x6 0.25 us: wide(): jnp.tile(jnp.repeat(values.reshape(1, -1), lag_count, axis=1), (1, 2))]
    dot_general x3 -> x0, matrix products: 10.1 us -> none  [the longest x1 4.43 us: shards(): lax.dot_general(spread, high, (((0,), (0,)), ((), ())), preferred_element...]
  transfers between devices with their start and end apart: 2 -> 0, of which waited for: 1 -> 0; matrix products, arithmetic and copies ran while one was open for 14% -> 0% of each run, Pallas kernels for 0% -> 0%
where the time goes in v2:
time: 108 us
  Pallas kernels  97.2 us (90%)
  local copies, waits for them, and re-layouts  9.97 us (9%)
    pallas_call x1, Pallas kernels, shards(): pl.pallas_call(functools.partial(kernel, nz, nobs, hour_count), out_shape...  97.2 us
    reshape x2, local copies, waits for them, and re-layouts, shards(): footprint.reshape(block_count, slot_width, sounding_count * lag_count, no...  7 us

profile of v2, /device:TPU:8, one launch (start us, length us, event | category | flops | bytes accessed | tf_op | source)
XLA Modules:
  0.0 108.2 jit_solution(17648794186985350279)
XLA Ops:
  0.6 4.5 %reshape.96 = bf16[8,4,8,32,128]{4,3,2,1,0:T(8,128)(2,1)} reshape(bf16[8,4,4,2,4096]{4,3,2,1,0:T(2,128)(2,1)} %param.7) | data formatting | bytes 4194304 | tf_op jit(solution)/shard_map/reshape | solution.py:313
  5.1 0.0 copy-start.5
  5.1 0.0 copy-start.1
  5.1 0.0 copy-start.2
  5.1 0.0 copy-start.3
  5.1 0.0 copy-start.4
  5.1 0.0 copy-start
  5.2 2.5 %copy.27 = bf16[8,4,8,32,128]{4,2,0,1,3:T(8,128)(2,1)S(1)} copy(bf16[8,4,8,32,128]{4,3,2,1,0:T(8,128)(2,1)} %reshape.96) | data formatting | bytes 4194304 | tf_op jit(solution)/shard_map/reshape | solution.py:313
  7.7 0.0 copy-done.5
  7.7 0.1 copy.22
  7.8 0.1 reshape.98
  7.9 0.1 broadcast_in_dim.29
  7.9 0.1 broadcast_in_dim.30
  8.0 0.1 tile.34
  8.1 0.0 copy-done.1
  8.1 0.1 copy.23
  8.2 0.1 reshape.99
  8.3 0.1 broadcast_in_dim.31
  8.4 0.1 broadcast_in_dim.32
  8.5 0.1 tile.36
  8.6 0.0 copy-done.2
  8.6 0.1 copy.24
  8.7 0.1 reshape.100
  8.8 0.1 broadcast_in_dim.33
  8.8 0.1 broadcast_in_dim.34
  8.9 0.1 tile.38
  9.0 0.0 copy-done.3
  9.0 0.0 copy-done.4
  9.0 0.2 select_reduce_fusion
  9.3 0.1 tile.40
  9.4 0.0 copy-done
  9.4 97.2 %transport.1 = (f32[8,128]{1,0:T(8,128)S(1)}, f32[5,32,128]{2,1,0:T(8,128)S(1)}) custom-call(bf16[32,4,64,128]{3,2,1,0:T(8,128)(2,1)S(1)} %bitcast.11, bf16[5,32,4096]{2,1,0:T(8,128)(2,1)S(1)} %bitcast.12, f32[8,128]{1,0:T(8,128)S(1)} %concatenate.3.meta), custom_call_target="tpu_custom_call" | custom-call | tf_op jit(solution)/shard_map/transport/pallas_call | solution.py:320
  106.7 0.1 dynamic-slice_reduce_fusion
  106.7 0.1 reshape.101
  106.9 0.7 copy.25
  107.5 0.6 copy.29
  (10 shorter events, 0.1 us)
Async XLA Ops:
  5.1 2.5 %copy-start.5 = (s32[8,4]{0,1:T(4,128)S(1)}, s32[8,4]{0,1:T(4,128)}, u32[]{:S(2)}) copy-start(s32[8,4]{0,1:T(4,128)} %param.8) | copy-start | bytes 388
  5.1 3.0 %copy-start.1 = (f32[8,4]{0,1:T(4,128)S(1)}, f32[8,4]{0,1:T(4,128)}, u32[]{:S(2)}) copy-start(f32[8,4]{0,1:T(4,128)} %param.12) | copy-start | bytes 388
  5.1 3.5 %copy-start.2 = (f32[8,4]{0,1:T(4,128)S(1)}, f32[8,4]{0,1:T(4,128)}, u32[]{:S(2)}) copy-start(f32[8,4]{0,1:T(4,128)} %param.13) | copy-start | bytes 388
  5.1 3.9 %copy-start.3 = (s32[512]{0:T(512)S(1)}, s32[512]{0:T(512)}, u32[]{:S(2)}) copy-start(s32[512]{0:T(512)} %param.10) | copy-start | bytes 6148
  5.1 3.9 %copy-start.4 = (s32[8,4]{0,1:T(4,128)S(1)}, s32[8,4]{0,1:T(4,128)}, u32[]{:S(2)}) copy-start(s32[8,4]{0,1:T(4,128)} %param.9) | copy-start | bytes 388
  5.1 4.3 %copy-start = (bf16[32,5,4096]{2,0,1:T(8,128)(2,1)S(1)}, bf16[32,5,4096]{2,0,1:T(8,128)(2,1)}, u32[]{:S(2)}) copy-start(bf16[32,5,4096]{2,0,1:T(8,128)(2,1)} %param.11) | copy-start | bytes 3932164

commit v3 on v2

v3 whole, which is shorter than its diff:
```python
import functools

import jax
import jax.numpy as jnp
from jax import lax
from jax.experimental import pallas as pl
from jax.experimental.pallas import tpu as pltpu
from jax.sharding import PartitionSpec as P

MESH = pl.DeviceIdType.MESH
LANES = 128
ROW = 4
PIECES = ((0, 3), (3, 2))


def kernel(
    nz, nobs, hours, feet, flux, hour_in, row_in, seen_in, var_in, mod, grad,
    held, wide, window, own, metas, pairs, onehot, spread, near, parts, total, high, low,
    mine, down, down_leaf, up, up_leaf,
    local_sem, tree_send, tree_recv, meta_send, meta_recv, feet_send, feet_recv,
    part_send, part_recv, sum_send, sum_recv,
):
    f32, bf16 = jnp.float32, jnp.bfloat16
    chips = nobs // 2
    tiles = flux.shape[1]
    count = nz * tiles
    blocks = feet.shape[0]
    width = 2 * blocks
    slots = chips * width
    depth = nz // 4
    z = lax.axis_index("flux")
    me = lax.axis_index("obs")
    chip, core = me // 2, lax.rem(me, 2)
    y, x = chip // ROW, lax.rem(chip, ROW)

    def level(d):
        return lax.rem(z + d + 2 * nz, nz)

    def target(t):
        c = t // 2
        there = lax.rem(y + c // ROW, chips // ROW) * ROW + lax.rem(x + lax.rem(c, ROW), ROW)
        return there * 2 + lax.rem(core + t, 2)

    def source_chip(c):
        return lax.rem(y + chips // ROW - c // ROW, chips // ROW) * ROW + lax.rem(
            x + ROW - lax.rem(c, ROW), ROW
        )

    def source(t):
        return source_chip(t // 2) * 2 + lax.rem(core + t, 2)

    def remote(src, dst, send, recv, to):
        return pltpu.make_async_remote_copy(
            src_ref=src, dst_ref=dst, send_sem=send, recv_sem=recv,
            device_id=to, device_id_type=MESH,
        )

    def cells(i):
        return feet.at[:, :, :, :, pl.ds(pl.multiple_of(i * LANES, LANES), LANES)]

    def feet_copy(t, i):
        to = target(t)
        return remote(
            cells(to), held.at[i // 2, lax.rem(i, 2)], feet_send.at[t], feet_recv.at[t], (z, to)
        )

    def meta_copy(t, i):
        return remote(own, metas.at[i], meta_send.at[t], meta_recv.at[t], (z, target(t)))

    def part_copy(t, i):
        return remote(parts.at[me], parts.at[i], part_send.at[t], part_recv.at[t], (z, target(t)))

    def tree_copy(kind, s, origin):
        at = window.at[:, pl.ds(pl.multiple_of(origin * tiles, tiles), tiles), :]
        to = level((2, 1, -2, -1)[kind])
        return remote(at, at, tree_send.at[kind, s], tree_recv.at[kind, s], (to, me))

    def tree_start(s):
        tree_copy(0, s, level(-2 * s)).start()
        tree_copy(1, s, level(-2 * s)).start()
        if s < depth - 1:
            tree_copy(2, s, level(2 * s)).start()
        tree_copy(3, s, level(2 * s)).start()

    def tree_step(s):
        tree_copy(0, s - 1, level(-2 * s)).wait_recv()
        tree_copy(2, s - 1, level(2 * s)).wait_recv()
        tree_start(s)

    own_feet = pltpu.make_async_copy(cells(me), held.at[chip, core], local_sem.at[0])
    own_flux = pltpu.make_async_copy(
        flux.at[:, :, pl.ds(pl.multiple_of(me * LANES, LANES), LANES)],
        window.at[:, pl.ds(pl.multiple_of(z * tiles, tiles), tiles), :],
        local_sem.at[1],
    )
    own_flux.start()
    own_feet.start()

    barrier = pltpu.get_barrier_semaphore()
    for d in (1, -1, 2, -2):
        pl.semaphore_signal(barrier, inc=1, device_id=(level(d), me), device_id_type=MESH)

    @pl.loop(1, nobs)
    def _(t):
        pl.semaphore_signal(barrier, inc=1, device_id=(z, target(t)), device_id_type=MESH)

    lane4 = lax.broadcasted_iota(jnp.int32, (4, LANES), 1)
    sub4 = lax.broadcasted_iota(jnp.int32, (4, LANES), 0)

    def expand(values, block_at):
        result = jnp.zeros((4, LANES), f32)
        for b in range(blocks):
            result = jnp.where(block_at == b, values[:, b : b + 1], result)
        return result

    def in_row(values):
        chosen = sub4 == lax.rem(lane4 // 2, 4)
        spread_out = expand(values, lax.rem(lane4 // 8, blocks))
        return jnp.sum(jnp.where(chosen, spread_out, 0.0), axis=0, keepdims=True)

    lag = lax.rem(lane4[0:1], 2).astype(f32)
    own[0:1, :] = in_row(hour_in[...].astype(f32)) + lag
    own[1:2, :] = in_row(seen_in[...])
    own[2:3, :] = in_row(var_in[...])
    own[3:4, :] = jnp.zeros((1, LANES), f32)
    own[4:8, :] = expand(row_in[...], lax.rem(lane4, blocks))
    metas[me] = own[...]
    own_flux.wait()
    pl.semaphore_wait(barrier, nobs + 3)

    tree_start(0)

    @pl.loop(1, nobs)
    def _(t):
        meta_copy(t, me).start()

    @pl.loop(1, nobs)
    def _(t):
        feet_copy(t, me).start()

    if depth > 1:
        tree_step(1)

    @pl.loop(1, nobs)
    def _(t):
        meta_copy(t, source(t)).wait_recv()

    lane = lax.broadcasted_iota(jnp.int32, (8, LANES), 1)
    per_half = nobs // 2
    halves = []
    for half in range(2):
        gathered = jnp.zeros((8, LANES), f32)
        for i in range(per_half):
            gathered = jnp.where(lane // blocks == i, metas[half * per_half + i], gathered)
        halves.append(gathered)

    @pl.loop(0, chips)
    def _(g):
        pairs[g] = jnp.where(lane < 64, metas[2 * g], metas[2 * g + 1])

    for half in range(2):
        upright = halves[half].T
        for k in range(4):
            at = k * slots + half * LANES
            along = upright[:, 4 + k : 5 + k]
            tile_on = lax.broadcasted_iota(jnp.int32, (LANES, count), 1).astype(f32)
            onehot[at : at + LANES, :] = jnp.where(tile_on == along, 1.0, 0.0).astype(bf16)
    if depth > 2:
        tree_step(2)
    for half in range(2):
        for k in range(4):
            at = k * slots + half * LANES
            across = halves[half][4 + k : 5 + k, :]
            tile_at = lax.broadcasted_iota(jnp.int32, (count, LANES), 0).astype(f32)
            spread[:, at : at + LANES] = jnp.where(tile_at == across, 1.0, 0.0).astype(bf16)
    for s in range(3, depth):
        tree_step(s)
    tree_copy(0, depth - 1, level(-2 * depth)).wait_recv()
    for s in range(depth):
        tree_copy(1, s, level(-1 - 2 * s)).wait_recv()
        tree_copy(3, s, level(1 + 2 * s)).wait_recv()

    @pl.loop(0, 4)
    def _(k):
        begin = pl.multiple_of(k * slots, LANES)
        pick = onehot[pl.ds(begin, slots), :]
        for h in range(hours):
            near[h, pl.ds(begin, slots), :] = jnp.dot(
                pick, window[h], preferred_element_type=f32
            ).astype(bf16)

    mask_row = lax.broadcasted_iota(jnp.int32, (hours * width, LANES), 0)
    mask_lane = lax.broadcasted_iota(jnp.int32, (hours * width, LANES), 1)
    same_block = lax.rem(mask_row, width) == mask_lane // 8
    hour_of = (mask_row // width).astype(f32)

    def mask(g):
        return same_block & (hour_of == pairs[g, 0:1, :])

    own_feet.wait()

    @pl.loop(0, chips)
    def _(c):
        @pl.when(c > 0)
        def _():
            feet_copy(2 * c, source(2 * c)).wait_recv()

        feet_copy(2 * c + 1, source(2 * c + 1)).wait_recv()
        g = source_chip(c)
        here = jnp.concatenate(
            [held[g, :, :, k].reshape(LANES, LANES) for k in range(4)], axis=1
        )
        wide[g] = here
        flux_rows = []
        for k in range(4):
            begin = pl.multiple_of(k * slots + g * width, width)
            flux_rows.append(
                jnp.concatenate([near[h, pl.ds(begin, width), :] for h in range(hours)], axis=0)
            )
        products = lax.dot_general(
            jnp.concatenate(flux_rows, axis=1), here,
            (((1,), (1,)), ((), ())), preferred_element_type=f32,
        )
        parts[me, pl.ds(g, 1), :] = jnp.sum(
            jnp.where(mask(g), products, 0.0), axis=0, keepdims=True
        )

    @pl.loop(1, nobs)
    def _(t):
        part_copy(t, me).start()

    @pl.loop(1, nobs)
    def _(t):
        part_copy(t, source(t)).wait_recv()

    summed = parts[0]
    for i in range(1, nobs):
        summed = summed + parts[i]
    even = lax.rem(lax.broadcasted_iota(jnp.int32, (chips, LANES), 1), 2) == 0
    total[...] = summed + jnp.where(
        even, pltpu.roll(summed, LANES - 1, 1), pltpu.roll(summed, 1, 1)
    )
    mod[...] = jnp.broadcast_to(total[pl.ds(chip, 1), :], mod.shape)

    @pl.loop(0, chips)
    def _(g):
        misfit = (total[pl.ds(g, 1), :] - pairs[g, 1:2, :]) / pairs[g, 2:3, :]
        scaled = misfit.astype(bf16).astype(f32)
        coefficient = jnp.where(mask(g), scaled, 0.0).astype(bf16)
        terms = jnp.dot(coefficient, wide[g], preferred_element_type=f32)
        upper = terms.astype(bf16)
        lower = (terms - upper.astype(f32)).astype(bf16)
        for k in range(4):
            begin = pl.multiple_of(k * slots + g * width, width)
            for h in range(hours):
                cut = (slice(h * width, (h + 1) * width), slice(k * LANES, (k + 1) * LANES))
                high[pl.ds(begin, width), h * LANES : (h + 1) * LANES] = upper[cut]
                low[pl.ds(begin, width), h * LANES : (h + 1) * LANES] = lower[cut]

    several = LANES // tiles
    lots = count // LANES

    def gradient_rows(q):
        pick = spread[pl.ds(pl.multiple_of(q * LANES, LANES), LANES), :]
        rows = jnp.dot(pick, high[...], preferred_element_type=f32) + jnp.dot(
            pick, low[...], preferred_element_type=f32
        )
        for i in range(several):
            for h in range(hours):
                mine[q * several + i, h] = rows[
                    i * tiles : (i + 1) * tiles, h * LANES : (h + 1) * LANES
                ]

    top = 2 * depth

    def sum_copy(kind, s, p):
        h = pl.ds(PIECES[p][0], PIECES[p][1])
        if kind == 0:
            src = mine.at[level(-top), h] if s == 0 else down.at[s - 1, h]
            dst, to = down.at[s, h], level(-2)
        elif kind == 1:
            src, dst, to = mine.at[level(1 - top + 2 * s), h], down_leaf.at[s, h], level(-1)
        elif kind == 2:
            src, dst, to = up_leaf.at[s, h], up.at[s, h], level(2)
        else:
            src, dst, to = mine.at[level(top - 1 - 2 * s), h], up_leaf.at[s, h], level(1)
        return remote(src, dst, sum_send.at[kind, s, p], sum_recv.at[kind, s, p], (to, me))

    first = level(top) // several
    gradient_rows(first)
    for p in range(len(PIECES)):
        sum_copy(0, 0, p).start()
    if lots > 1:
        @pl.loop(1, lots)
        def _(j):
            gradient_rows(lax.rem(first + j, lots))

    for p in range(len(PIECES)):
        sum_copy(3, 0, p).start()
        sum_copy(1, 0, p).start()
    for s in range(1, depth):
        for p in range(len(PIECES)):
            h = pl.ds(PIECES[p][0], PIECES[p][1])
            sum_copy(3, s - 1, p).wait_recv()
            add = mine[level(top - 2 * s), h]
            if s > 1:
                sum_copy(2, s - 2, p).wait_recv()
                add = add + up[s - 2, h]
            up_leaf[s - 1, h] += add
            sum_copy(2, s - 1, p).start()
        for p in range(len(PIECES)):
            h = pl.ds(PIECES[p][0], PIECES[p][1])
            sum_copy(1, s - 1, p).wait_recv()
            add = mine[level(2 * s - top), h] + down_leaf[s - 1, h]
            sum_copy(0, s - 1, p).wait_recv()
            down[s - 1, h] += add
            sum_copy(0, s, p).start()
        for p in range(len(PIECES)):
            sum_copy(3, s, p).start()
            sum_copy(1, s, p).start()
    for p in range(len(PIECES)):
        h = pl.ds(PIECES[p][0], PIECES[p][1])
        sum_copy(3, depth - 1, p).wait_recv()
        sum_copy(1, depth - 1, p).wait_recv()
        value = mine[z, h] + up_leaf[depth - 1, h] + down_leaf[depth - 1, h]
        if depth > 1:
            sum_copy(2, depth - 2, p).wait_recv()
            value = value + up[depth - 2, h]
        sum_copy(0, depth - 1, p).wait_recv()
        grad[h] = value + down[depth - 1, h]

    for s in range(depth):
        for kind in range(4):
            if kind == 2 and s == depth - 1:
                continue
            tree_copy(kind, s, z).wait_send()
            for p in range(len(PIECES)):
                sum_copy(kind, s, p).wait_send()

    @pl.loop(1, nobs)
    def _(t):
        meta_copy(t, me).wait_send()
        feet_copy(t, me).wait_send()
        part_copy(t, me).wait_send()


def shards(footprint, obs_hour, tile_list, tile_row, flux, observed, obs_var):
    nobs, nz = lax.axis_size("obs"), lax.axis_size("flux")
    block_count, slot_width, sounding_count, lag_count, cell_count = footprint.shape
    tile_count, hour_count, _ = flux.shape
    me = lax.axis_index("obs")
    f32, bf16 = jnp.float32, jnp.bfloat16
    table_hits = tile_list[..., None] == jnp.arange(tile_row.shape[0], dtype=jnp.int32)
    storage = jnp.sum(jnp.where(table_hits, tile_row, 0), axis=-1).astype(f32)
    chips, count, slots = nobs // 2, nz * tile_count, nobs * block_count
    depth = nz // 4
    chunk = (hour_count, tile_count, LANES)
    dma = pltpu.SemaphoreType.DMA
    vmem = pl.BlockSpec(memory_space=pltpu.VMEM)
    mod, grad = pl.pallas_call(
        functools.partial(kernel, nz, nobs, hour_count),
        out_shape=(
            jax.ShapeDtypeStruct((8, LANES), f32),
            jax.ShapeDtypeStruct(chunk, f32),
        ),
        in_specs=[pl.BlockSpec(memory_space=pl.ANY)] * 2 + [vmem] * 4,
        out_specs=(vmem,) * 2,
        scratch_shapes=[
            pltpu.VMEM((chips, 2) + footprint.shape[:4] + (LANES,), bf16),
            pltpu.VMEM((chips, LANES, slot_width * LANES), bf16),
            pltpu.VMEM((hour_count, count, LANES), bf16),
            pltpu.VMEM((8, LANES), f32),
            pltpu.VMEM((nobs, 8, LANES), f32),
            pltpu.VMEM((chips, 8, LANES), f32),
            pltpu.VMEM((slots * slot_width, count), bf16),
            pltpu.VMEM((count, slots * slot_width), bf16),
            pltpu.VMEM((hour_count, slots * slot_width, LANES), bf16),
            pltpu.VMEM((nobs, chips, LANES), f32),
            pltpu.VMEM((chips, LANES), f32),
            pltpu.VMEM((slots * slot_width, hour_count * LANES), bf16),
            pltpu.VMEM((slots * slot_width, hour_count * LANES), bf16),
            pltpu.VMEM((nz,) + chunk, f32),
            pltpu.VMEM((depth,) + chunk, f32),
            pltpu.VMEM((depth,) + chunk, f32),
            pltpu.VMEM((depth,) + chunk, f32),
            pltpu.VMEM((depth,) + chunk, f32),
            dma((2,)),
            dma((4, depth)),
            dma((4, depth)),
            dma((nobs,)),
            dma((nobs,)),
            dma((nobs,)),
            dma((nobs,)),
            dma((nobs,)),
            dma((nobs,)),
            dma((4, depth, len(PIECES))),
            dma((4, depth, len(PIECES))),
        ],
        compiler_params=pltpu.CompilerParams(
            collective_id=0, has_side_effects=True, vmem_limit_bytes=40 << 20
        ),
        name="transport",
    )(footprint, flux.transpose(1, 0, 2), obs_hour.T, storage.T, observed.T, obs_var.T)
    mine = lax.dynamic_slice_in_dim(mod[0], lax.rem(me, 2) * 64, 64)
    modeled = mine.reshape(block_count, sounding_count, lag_count)[:, :, 0]
    return modeled, grad.transpose(1, 0, 2)


def solution(mesh):
    placed = (
        P(("flux", "obs"), None, None, None, None),
        P(("flux", "obs"), None),
        P(("flux", "obs"), None),
        P(),
        P("flux", None, None),
        P(("flux", "obs"), None),
        P(("flux", "obs"), None),
    )
    return jax.shard_map(
        shards,
        mesh=mesh,
        in_specs=placed,
        out_specs=(P(("flux", "obs"), None), P("flux", None, "obs")),
        check_vma=False,
    )
```

time: 108 us -> 97.3 us (0.901)
  Pallas kernels: 97.2 us -> 88.9 us
  local copies, waits for them, and re-layouts: 9.97 us -> 6.48 us
    pallas_call x1, Pallas kernels: 97.2 us -> 88.9 us  [shards(): pl.pallas_call(functools.partial(kernel, nz, nobs, hour_count), out_shape...]
    reshape x6 -> x1, local copies, waits for them, and re-layouts: 7.35 us -> 0.11 us  [shards(): modeled = mine.reshape(block_count, sounding_count, lag_count)[:, :, 0]]
    unnamed x15 -> x11, local copies, waits for them, and re-layouts: 0.82 us -> 5.58 us
where the time goes in v3:
time: 97.3 us; the launch traced here: 97 us
  Pallas kernels  88.9 us (91%)
  local copies, waits for them, and re-layouts  6.48 us (7%)
    pallas_call x1, Pallas kernels, shards(): pl.pallas_call(functools.partial(kernel, nz, nobs, hour_count), out_shape...  88.9 us
    unnamed x11, local copies, waits for them, and re-layouts  5.58 us

profile of v3, /device:TPU:8, one launch (start us, length us, event | category | flops | bytes accessed | tf_op | source)
XLA Modules:
  0.0 97.0 jit_solution(3739888033009428129)
XLA Ops:
  0.6 0.9 select_reduce_fusion
  1.6 0.0 copy-start
  1.6 1.6 %copy-done = bf16[8,4,4,2,4096]{4,3,2,1,0:T(2,128)(2,1)S(1)} copy-done((bf16[8,4,4,2,4096]{4,3,2,1,0:T(2,128)(2,1)S(1)}, bf16[8,4,4,2,4096]{4,3,2,1,0:T(2,128)(2,1)}, u32[]{:S(2)}) %copy-start) | copy-done | bytes 2097176
  3.2 0.0 copy-start.1
  3.2 1.3 %copy-done.1 = bf16[32,5,4096]{2,0,1:T(8,128)(2,1)S(1)} copy-done((bf16[32,5,4096]{2,0,1:T(8,128)(2,1)S(1)}, bf16[32,5,4096]{2,0,1:T(8,128)(2,1)}, u32[]{:S(2)}) %copy-start.1) | copy-done | bytes 1310744
  4.5 0.0 copy-start.2
  4.5 0.7 copy-done.2
  5.2 0.0 copy-start.3
  5.2 0.7 copy-done.3
  5.8 0.0 copy-start.4
  5.8 0.7 copy-done.4
  6.5 88.9 %transport.1 = (f32[8,128]{1,0:T(8,128)S(1)}, f32[5,32,128]{2,1,0:T(8,128)S(1)}) custom-call(bf16[8,4,4,2,4096]{4,3,2,1,0:T(2,128)(2,1)S(1)} %copy-done, bf16[5,32,4096]{2,1,0:T(8,128)(2,1)S(1)} %bitcast.9, s32[4,8]{1,0:T(4,128)S(1)} %bitcast.11, f32[4,8]{1,0:T(4,128)S(1)} %convert_bitcast_fusion.row_in, f32[4,8]{1,0:T(4,128)S(1)} %bitcast.12, ...), custom_call_target="tpu_custom_call" | custom-call | tf_op jit(solution)/shard_map/transport/pallas_call | solution.py:360
  95.4 0.1 dynamic-slice_reduce_fusion
  95.5 0.1 reshape.10
  95.7 0.7 copy.13
  96.3 0.6 copy.15
  (2 shorter events, 0.0 us)
Async XLA Ops:
  1.6 1.6 %copy-start = (bf16[8,4,4,2,4096]{4,3,2,1,0:T(2,128)(2,1)S(1)}, bf16[8,4,4,2,4096]{4,3,2,1,0:T(2,128)(2,1)}, u32[]{:S(2)}) copy-start(bf16[8,4,4,2,4096]{4,3,2,1,0:T(2,128)(2,1)} %feet.1) | copy-start | bytes 6291460
  3.2 1.3 %copy-start.1 = (bf16[32,5,4096]{2,0,1:T(8,128)(2,1)S(1)}, bf16[32,5,4096]{2,0,1:T(8,128)(2,1)}, u32[]{:S(2)}) copy-start(bf16[32,5,4096]{2,0,1:T(8,128)(2,1)} %param.11) | copy-start | bytes 3932164
  4.5 0.7 copy-start.2
  5.2 0.7 copy-start.3
  5.8 0.7 copy-start.4

commit v4 on v3

--- a/solution.py
+++ b/solution.py
@@ -11,11 +11,12 @@
 LANES = 128
 ROW = 4
 PIECES = ((0, 3), (3, 2))
+STRIDE = 7
 
 
 def kernel(
-    nz, nobs, hours, feet, flux, hour_in, row_in, seen_in, var_in, mod, grad,
-    held, wide, window, own, metas, pairs, onehot, spread, near, parts, total, high, low,
+    nz, nobs, hours, feet, flux, hour_hbm, list_hbm, row_hbm, seen_hbm, var_hbm, mod, grad,
+    hour_in, list_in, row_in, seen_in, var_in, held, wide, window, own, metas, pairs, onehot, spread, near, parts, total, high, low,
     mine, down, down_leaf, up, up_leaf,
     local_sem, tree_send, tree_recv, meta_send, meta_recv, feet_send, feet_recv,
     part_send, part_recv, sum_send, sum_recv,
@@ -33,8 +34,10 @@
     chip, core = me // 2, lax.rem(me, 2)
     y, x = chip // ROW, lax.rem(chip, ROW)
 
+    side = 1 - 2 * core
+
     def level(d):
-        return lax.rem(z + d + 2 * nz, nz)
+        return lax.rem(z + side * d + 2 * nz, nz)
 
     def target(t):
         c = t // 2
@@ -93,7 +96,21 @@
         window.at[:, pl.ds(pl.multiple_of(z * tiles, tiles), tiles), :],
         local_sem.at[1],
     )
+    small = [
+        pltpu.make_async_copy(src, dst, local_sem.at[2 + i])
+        for i, (src, dst) in enumerate(
+            [
+                (hour_hbm, hour_in),
+                (list_hbm, list_in),
+                (row_hbm, row_in),
+                (seen_hbm, seen_in),
+                (var_hbm, var_in),
+            ]
+        )
+    ]
     own_flux.start()
+    for copy in small:
+        copy.start()
     own_feet.start()
 
     barrier = pltpu.get_barrier_semaphore()
@@ -107,15 +124,19 @@
     lane4 = lax.broadcasted_iota(jnp.int32, (4, LANES), 1)
     sub4 = lax.broadcasted_iota(jnp.int32, (4, LANES), 0)
 
-    def expand(values, block_at):
+    for copy in small:
+        copy.wait()
+
+    def expand(columns, block_at):
         result = jnp.zeros((4, LANES), f32)
         for b in range(blocks):
-            result = jnp.where(block_at == b, values[:, b : b + 1], result)
+            result = jnp.where(block_at == b, columns[b], result)
         return result
 
     def in_row(values):
         chosen = sub4 == lax.rem(lane4 // 2, 4)
-        spread_out = expand(values, lax.rem(lane4 // 8, blocks))
+        columns = [values[:, b : b + 1] for b in range(blocks)]
+        spread_out = expand(columns, lax.rem(lane4 // 8, blocks))
         return jnp.sum(jnp.where(chosen, spread_out, 0.0), axis=0, keepdims=True)
 
     lag = lax.rem(lane4[0:1], 2).astype(f32)
@@ -123,7 +144,18 @@
     own[1:2, :] = in_row(seen_in[...])
     own[2:3, :] = in_row(var_in[...])
     own[3:4, :] = jnp.zeros((1, LANES), f32)
-    own[4:8, :] = expand(row_in[...], lax.rem(lane4, blocks))
+    listed = list_in[...]
+    row_of = row_in[...].astype(f32)
+    table_at = lax.broadcasted_iota(jnp.int32, (4, row_of.shape[1]), 1)
+    own[4:8, :] = expand(
+        [
+            jnp.sum(
+                jnp.where(table_at == listed[:, b : b + 1], row_of, 0.0), axis=1, keepdims=True
+            )
+            for b in range(blocks)
+        ],
+        lax.rem(lane4, blocks),
+    )
     metas[me] = own[...]
     own_flux.wait()
     pl.semaphore_wait(barrier, nobs + 3)
@@ -134,9 +166,9 @@
     def _(t):
         meta_copy(t, me).start()
 
-    @pl.loop(1, nobs)
-    def _(t):
-        feet_copy(t, me).start()
+    @pl.loop(0, nobs - 1)
+    def _(i):
+        feet_copy(lax.rem(i * STRIDE, nobs - 1) + 1, me).start()
 
     if depth > 1:
         tree_step(1)
@@ -240,7 +272,6 @@
     total[...] = summed + jnp.where(
         even, pltpu.roll(summed, LANES - 1, 1), pltpu.roll(summed, 1, 1)
     )
-    mod[...] = jnp.broadcast_to(total[pl.ds(chip, 1), :], mod.shape)
 
     @pl.loop(0, chips)
     def _(g):
@@ -298,6 +329,16 @@
     for p in range(len(PIECES)):
         sum_copy(3, 0, p).start()
         sum_copy(1, 0, p).start()
+    here_row = jnp.broadcast_to(total[pl.ds(chip, 1), :], (4, LANES))
+    wanted = jnp.where(lane4 // 2 - (lane4 // 8) * 4 == sub4, here_row, 0.0)
+    answer = jnp.zeros((4, blocks), f32)
+    block_lane = lax.broadcasted_iota(jnp.int32, (4, blocks), 1)
+    for b in range(blocks):
+        at = (lane4 // 8 == core * blocks + b) & (lax.rem(lane4, 2) == 0)
+        picked = jnp.sum(jnp.where(at, wanted, 0.0), axis=1, keepdims=True)
+        answer = jnp.where(block_lane == b, picked, answer)
+    mod[...] = answer
+
     for s in range(1, depth):
         for p in range(len(PIECES)):
             h = pl.ds(PIECES[p][0], PIECES[p][1])
@@ -348,10 +389,7 @@
     nobs, nz = lax.axis_size("obs"), lax.axis_size("flux")
     block_count, slot_width, sounding_count, lag_count, cell_count = footprint.shape
     tile_count, hour_count, _ = flux.shape
-    me = lax.axis_index("obs")
     f32, bf16 = jnp.float32, jnp.bfloat16
-    table_hits = tile_list[..., None] == jnp.arange(tile_row.shape[0], dtype=jnp.int32)
-    storage = jnp.sum(jnp.where(table_hits, tile_row, 0), axis=-1).astype(f32)
     chips, count, slots = nobs // 2, nz * tile_count, nobs * block_count
     depth = nz // 4
     chunk = (hour_count, tile_count, LANES)
@@ -360,12 +398,17 @@
     mod, grad = pl.pallas_call(
         functools.partial(kernel, nz, nobs, hour_count),
         out_shape=(
-            jax.ShapeDtypeStruct((8, LANES), f32),
+            jax.ShapeDtypeStruct((sounding_count, block_count), f32),
             jax.ShapeDtypeStruct(chunk, f32),
         ),
-        in_specs=[pl.BlockSpec(memory_space=pl.ANY)] * 2 + [vmem] * 4,
+        in_specs=[pl.BlockSpec(memory_space=pltpu.HBM)] * 7,
         out_specs=(vmem,) * 2,
         scratch_shapes=[
+            pltpu.VMEM((sounding_count, block_count), jnp.int32),
+            pltpu.VMEM((slot_width, block_count), jnp.int32),
+            pltpu.VMEM((1, count), jnp.int32),
+            pltpu.VMEM((sounding_count, block_count), f32),
+            pltpu.VMEM((sounding_count, block_count), f32),
             pltpu.VMEM((chips, 2) + footprint.shape[:4] + (LANES,), bf16),
             pltpu.VMEM((chips, LANES, slot_width * LANES), bf16),
             pltpu.VMEM((hour_count, count, LANES), bf16),
@@ -384,7 +427,7 @@
             pltpu.VMEM((depth,) + chunk, f32),
             pltpu.VMEM((depth,) + chunk, f32),
             pltpu.VMEM((depth,) + chunk, f32),
-            dma((2,)),
+            dma((7,)),
             dma((4, depth)),
             dma((4, depth)),
             dma((nobs,)),
@@ -397,13 +440,14 @@
             dma((4, depth, len(PIECES))),
         ],
         compiler_params=pltpu.CompilerParams(
-            collective_id=0, has_side_effects=True, vmem_limit_bytes=40 << 20
+            collective_id=0, has_side_effects=True, vmem_limit_bytes=60 << 20
         ),
         name="transport",
-    )(footprint, flux.transpose(1, 0, 2), obs_hour.T, storage.T, observed.T, obs_var.T)
-    mine = lax.dynamic_slice_in_dim(mod[0], lax.rem(me, 2) * 64, 64)
-    modeled = mine.reshape(block_count, sounding_count, lag_count)[:, :, 0]
-    return modeled, grad.transpose(1, 0, 2)
+    )(
+        footprint, flux.transpose(1, 0, 2), obs_hour.T, tile_list.T,
+        tile_row.reshape(1, count), observed.T, obs_var.T,
+    )
+    return mod.T, grad.transpose(1, 0, 2)
 
 
 def solution(mesh):

time: 97.3 us -> 87.6 us (0.900)
  the two profiles are of different devices: /device:TPU:8 before, /device:TPU:1 now
where the time goes in v4:
time: 87.6 us; the launch traced here: 87.4 us
  Pallas kernels  84 us (96%)
  local copies, waits for them, and re-layouts  2.79 us (3%)
    pallas_call x1, Pallas kernels, shards(): pl.pallas_call(functools.partial(kernel, nz, nobs, hour_count), out_shape...  84 us
    unnamed x2, local copies, waits for them, and re-layouts  2.79 us

profile of v4, /device:TPU:1, one launch (start us, length us, event | category | flops | bytes accessed | tf_op | source)
XLA Modules:
  0.0 87.4 jit_solution(13625549231347611938)
XLA Ops:
  0.6 84.0 %transport.1 = (f32[4,8]{1,0:T(4,128)}, f32[5,32,128]{2,1,0:T(8,128)}) custom-call(bf16[8,4,4,2,4096]{4,3,2,1,0:T(2,128)(2,1)} %feet.1, bf16[5,32,4096]{2,1,0:T(8,128)(2,1)} %bitcast.8, s32[4,8]{1,0:T(4,128)} %bitcast.10, s32[4,8]{1,0:T(4,128)} %bitcast.11, s32[1,512]{1,0:T(1,128)} %bitcast.12, f32[4,8]{1,0:T(4,128)} %bitcast.13, f32[4,8]{1,0:T(4,128)} %bitcast.14), custom_call_target="tpu_custom_call" | custom-call | tf_op jit(solution)/shard_map/transport/pallas_call | solution.py:398
  84.6 1.3 %copy.11 = f32[8,4]{0,1:T(4,128)} copy(f32[8,4]{0,1:T(4,128)} %bitcast.15) | data formatting | bytes 256
  85.9 1.5 %copy.12 = f32[32,5,128]{2,0,1:T(8,128)} copy(f32[32,5,128]{2,0,1:T(8,128)} %bitcast.9) | data formatting | bytes 163840

commit v5 on v4

--- a/solution.py
+++ b/solution.py
@@ -10,8 +10,19 @@
 MESH = pl.DeviceIdType.MESH
 LANES = 128
 ROW = 4
-PIECES = ((0, 3), (3, 2))
-STRIDE = 7
+PIECES = ((0, 2), (2, 2), (4, 1))
+ORDER = (
+    4, 23, 18, 16, 1, 26, 5, 8, 15, 17, 21, 25, 13, 19, 11, 14,
+    24, 29, 7, 20, 9, 10, 22, 6, 12, 27, 3, 2, 30, 28, 31,
+)
+
+
+def hops(t):
+    c = t // 2
+    return sum(min(d, ROW - d) for d in (c // ROW, c % ROW))
+
+
+FAR = tuple(sorted(ORDER, key=hops, reverse=True))
 
 
 def kernel(
@@ -114,11 +125,10 @@
     own_feet.start()
 
     barrier = pltpu.get_barrier_semaphore()
-    for d in (1, -1, 2, -2):
+    for d in (2, -2, 1, -1):
         pl.semaphore_signal(barrier, inc=1, device_id=(level(d), me), device_id_type=MESH)
 
-    @pl.loop(1, nobs)
-    def _(t):
+    for t in FAR:
         pl.semaphore_signal(barrier, inc=1, device_id=(z, target(t)), device_id_type=MESH)
 
     lane4 = lax.broadcasted_iota(jnp.int32, (4, LANES), 1)
@@ -162,13 +172,11 @@
 
     tree_start(0)
 
-    @pl.loop(1, nobs)
-    def _(t):
+    for t in FAR:
         meta_copy(t, me).start()
 
-    @pl.loop(0, nobs - 1)
-    def _(i):
-        feet_copy(lax.rem(i * STRIDE, nobs - 1) + 1, me).start()
+    for t in ORDER:
+        feet_copy(t, me).start()
 
     if depth > 1:
         tree_step(1)
@@ -257,8 +265,7 @@
             jnp.where(mask(g), products, 0.0), axis=0, keepdims=True
         )
 
-    @pl.loop(1, nobs)
-    def _(t):
+    for t in FAR:
         part_copy(t, me).start()
 
     @pl.loop(1, nobs)
@@ -273,7 +280,7 @@
         even, pltpu.roll(summed, LANES - 1, 1), pltpu.roll(summed, 1, 1)
     )
 
-    @pl.loop(0, chips)
+    @pl.loop(0, chips, unroll=4)
     def _(g):
         misfit = (total[pl.ds(g, 1), :] - pairs[g, 1:2, :]) / pairs[g, 2:3, :]
         scaled = misfit.astype(bf16).astype(f32)
@@ -288,21 +295,22 @@
                 high[pl.ds(begin, width), h * LANES : (h + 1) * LANES] = upper[cut]
                 low[pl.ds(begin, width), h * LANES : (h + 1) * LANES] = lower[cut]
 
-    several = LANES // tiles
-    lots = count // LANES
-
-    def gradient_rows(q):
-        pick = spread[pl.ds(pl.multiple_of(q * LANES, LANES), LANES), :]
-        rows = jnp.dot(pick, high[...], preferred_element_type=f32) + jnp.dot(
-            pick, low[...], preferred_element_type=f32
-        )
-        for i in range(several):
-            for h in range(hours):
-                mine[q * several + i, h] = rows[
-                    i * tiles : (i + 1) * tiles, h * LANES : (h + 1) * LANES
-                ]
-
     top = 2 * depth
+
+    def gradient_hours(p):
+        begin, many = PIECES[p]
+        at = slice(begin * LANES, (begin + many) * LANES)
+
+        @pl.loop(0, count // LANES)
+        def _(q):
+            pick = spread[pl.ds(pl.multiple_of(q * LANES, LANES), LANES), :]
+            rows = jnp.dot(pick, high[:, at], preferred_element_type=f32) + jnp.dot(
+                pick, low[:, at], preferred_element_type=f32
+            )
+            for i in range(LANES // tiles):
+                for h in range(many):
+                    value = rows[i * tiles : (i + 1) * tiles, h * LANES : (h + 1) * LANES]
+                    mine[q * (LANES // tiles) + i, begin + h] = value
 
     def sum_copy(kind, s, p):
         h = pl.ds(PIECES[p][0], PIECES[p][1])
@@ -317,18 +325,12 @@
             src, dst, to = mine.at[level(top - 1 - 2 * s), h], up_leaf.at[s, h], level(1)
         return remote(src, dst, sum_send.at[kind, s, p], sum_recv.at[kind, s, p], (to, me))
 
-    first = level(top) // several
-    gradient_rows(first)
     for p in range(len(PIECES)):
+        gradient_hours(p)
         sum_copy(0, 0, p).start()
-    if lots > 1:
-        @pl.loop(1, lots)
-        def _(j):
-            gradient_rows(lax.rem(first + j, lots))
-
-    for p in range(len(PIECES)):
         sum_copy(3, 0, p).start()
         sum_copy(1, 0, p).start()
+
     here_row = jnp.broadcast_to(total[pl.ds(chip, 1), :], (4, LANES))
     wanted = jnp.where(lane4 // 2 - (lane4 // 8) * 4 == sub4, here_row, 0.0)
     answer = jnp.zeros((4, blocks), f32)

time: 87.6 us -> 83.2 us (0.950)
  Pallas kernels: 84 us -> 79.5 us
    pallas_call x1, Pallas kernels: 84 us -> 79.5 us  [shards(): pl.pallas_call(functools.partial(kernel, nz, nobs, hour_count), out_shape...]
where the time goes in v5:
time: 83.2 us; the launch traced here: 83 us
  Pallas kernels  79.5 us (96%)
  local copies, waits for them, and re-layouts  2.79 us (3%)
    pallas_call x1, Pallas kernels, shards(): pl.pallas_call(functools.partial(kernel, nz, nobs, hour_count), out_shape...  79.5 us
    unnamed x2, local copies, waits for them, and re-layouts  2.79 us

profile of v5, /device:TPU:1, one launch (start us, length us, event | category | flops | bytes accessed | tf_op | source)
XLA Modules:
  0.0 83.0 jit_solution(923495600733404888)
XLA Ops:
  0.6 79.5 %transport.1 = (f32[4,8]{1,0:T(4,128)}, f32[5,32,128]{2,1,0:T(8,128)}) custom-call(bf16[8,4,4,2,4096]{4,3,2,1,0:T(2,128)(2,1)} %feet.1, bf16[5,32,4096]{2,1,0:T(8,128)(2,1)} %bitcast.8, s32[4,8]{1,0:T(4,128)} %bitcast.10, s32[4,8]{1,0:T(4,128)} %bitcast.11, s32[1,512]{1,0:T(1,128)} %bitcast.12, f32[4,8]{1,0:T(4,128)} %bitcast.13, f32[4,8]{1,0:T(4,128)} %bitcast.14), custom_call_target="tpu_custom_call" | custom-call | tf_op jit(solution)/shard_map/transport/pallas_call | solution.py:400
  80.2 1.3 %copy.11 = f32[8,4]{0,1:T(4,128)} copy(f32[8,4]{0,1:T(4,128)} %bitcast.15) | data formatting | bytes 256
  81.4 1.5 %copy.12 = f32[32,5,128]{2,0,1:T(8,128)} copy(f32[32,5,128]{2,0,1:T(8,128)} %bitcast.9) | data formatting | bytes 163840

commit v6 on v5

--- a/solution.py
+++ b/solution.py
@@ -341,6 +341,16 @@
         answer = jnp.where(block_lane == b, picked, answer)
     mod[...] = answer
 
+    @pl.loop(1, nobs)
+    def _(t):
+        meta_copy(t, me).wait_send()
+        feet_copy(t, me).wait_send()
+        part_copy(t, me).wait_send()
+
+    for kind in range(4):
+        for s in range(depth - 1 if kind == 2 else depth):
+            tree_copy(kind, s, z).wait_send()
+
     for s in range(1, depth):
         for p in range(len(PIECES)):
             h = pl.ds(PIECES[p][0], PIECES[p][1])
@@ -361,6 +371,9 @@
         for p in range(len(PIECES)):
             sum_copy(3, s, p).start()
             sum_copy(1, s, p).start()
+        for kind in range(4):
+            for p in range(len(PIECES)):
+                sum_copy(kind, s - 1, p).wait_send()
     for p in range(len(PIECES)):
         h = pl.ds(PIECES[p][0], PIECES[p][1])
         sum_copy(3, depth - 1, p).wait_recv()
@@ -372,19 +385,9 @@
         sum_copy(0, depth - 1, p).wait_recv()
         grad[h] = value + down[depth - 1, h]
 
-    for s in range(depth):
-        for kind in range(4):
-            if kind == 2 and s == depth - 1:
-                continue
-            tree_copy(kind, s, z).wait_send()
-            for p in range(len(PIECES)):
-                sum_copy(kind, s, p).wait_send()
-
-    @pl.loop(1, nobs)
-    def _(t):
-        meta_copy(t, me).wait_send()
-        feet_copy(t, me).wait_send()
-        part_copy(t, me).wait_send()
+    for kind in (0, 1, 3):
+        for p in range(len(PIECES)):
+            sum_copy(kind, depth - 1, p).wait_send()
 
 
 def shards(footprint, obs_hour, tile_list, tile_row, flux, observed, obs_var):

time: 83.2 us -> 82.7 us (level)
  no operation moved by 1% of the time
where the time goes in v6:
time: 82.7 us; the launch traced here: 82.5 us
  Pallas kernels  79.1 us (96%)
  local copies, waits for them, and re-layouts  2.79 us (3%)
    pallas_call x1, Pallas kernels, shards(): pl.pallas_call(functools.partial(kernel, nz, nobs, hour_count), out_shape...  79.1 us
    unnamed x2, local copies, waits for them, and re-layouts  2.79 us

profile of v6, /device:TPU:1, one launch (start us, length us, event | category | flops | bytes accessed | tf_op | source)
XLA Modules:
  0.0 82.5 jit_solution(5015147328443433983)
XLA Ops:
  0.6 79.1 %transport.1 = (f32[4,8]{1,0:T(4,128)}, f32[5,32,128]{2,1,0:T(8,128)}) custom-call(bf16[8,4,4,2,4096]{4,3,2,1,0:T(2,128)(2,1)} %feet.1, bf16[5,32,4096]{2,1,0:T(8,128)(2,1)} %bitcast.8, s32[4,8]{1,0:T(4,128)} %bitcast.10, s32[4,8]{1,0:T(4,128)} %bitcast.11, s32[1,512]{1,0:T(1,128)} %bitcast.12, f32[4,8]{1,0:T(4,128)} %bitcast.13, f32[4,8]{1,0:T(4,128)} %bitcast.14), custom_call_target="tpu_custom_call" | custom-call | tf_op jit(solution)/shard_map/transport/pallas_call | solution.py:403
  79.7 1.3 %copy.11 = f32[8,4]{0,1:T(4,128)} copy(f32[8,4]{0,1:T(4,128)} %bitcast.15) | data formatting | bytes 256
  81.0 1.5 %copy.12 = f32[32,5,128]{2,0,1:T(8,128)} copy(f32[32,5,128]{2,0,1:T(8,128)} %bitcast.9) | data formatting | bytes 163840

commit v7 on v6

--- a/solution.py
+++ b/solution.py
@@ -22,6 +22,9 @@
     return sum(min(d, ROW - d) for d in (c // ROW, c % ROW))
 
 
+ARRIVAL = tuple(
+    sorted(range(16), key=lambda c: max(ORDER.index(max(2 * c, 1)), ORDER.index(2 * c + 1)))
+)
 FAR = tuple(sorted(ORDER, key=hops, reverse=True))
 
 
@@ -239,12 +242,9 @@
 
     own_feet.wait()
 
-    @pl.loop(0, chips)
-    def _(c):
-        @pl.when(c > 0)
-        def _():
+    for c in ARRIVAL:
+        if c > 0:
             feet_copy(2 * c, source(2 * c)).wait_recv()
-
         feet_copy(2 * c + 1, source(2 * c + 1)).wait_recv()
         g = source_chip(c)
         here = jnp.concatenate(

time: 82.7 us -> 82.8 us (level)
  no operation moved by 1% of the time
where the time goes in v7:
time: 82.8 us; the launch traced here: 82.5 us
  Pallas kernels  79.1 us (96%)
  local copies, waits for them, and re-layouts  2.79 us (3%)
    pallas_call x1, Pallas kernels, shards(): pl.pallas_call(functools.partial(kernel, nz, nobs, hour_count), out_shape...  79.1 us
    unnamed x2, local copies, waits for them, and re-layouts  2.79 us

profile of v7, /device:TPU:1, one launch (start us, length us, event | category | flops | bytes accessed | tf_op | source)
XLA Modules:
  0.0 82.5 jit_solution(4725182673577988464)
XLA Ops:
  0.6 79.1 %transport.1 = (f32[4,8]{1,0:T(4,128)}, f32[5,32,128]{2,1,0:T(8,128)}) custom-call(bf16[8,4,4,2,4096]{4,3,2,1,0:T(2,128)(2,1)} %feet.1, bf16[5,32,4096]{2,1,0:T(8,128)(2,1)} %bitcast.8, s32[4,8]{1,0:T(4,128)} %bitcast.10, s32[4,8]{1,0:T(4,128)} %bitcast.11, s32[1,512]{1,0:T(1,128)} %bitcast.12, f32[4,8]{1,0:T(4,128)} %bitcast.13, f32[4,8]{1,0:T(4,128)} %bitcast.14), custom_call_target="tpu_custom_call" | custom-call | tf_op jit(solution)/shard_map/transport/pallas_call | solution.py:403
  79.8 1.3 %copy.11 = f32[8,4]{0,1:T(4,128)} copy(f32[8,4]{0,1:T(4,128)} %bitcast.15) | data formatting | bytes 256
  81.0 1.5 %copy.12 = f32[32,5,128]{2,0,1:T(8,128)} copy(f32[32,5,128]{2,0,1:T(8,128)} %bitcast.9) | data formatting | bytes 163840
